TPU v7x, 32 devices: a whole 2x2x4 slice. The times are simulated.
32 devices in a mesh: dp: 2 (over core), row: 4 (over y, x), col: 4 (over z).
Axes of the slice: x: 2, y: 2, z: 4, core: 2. Of those that a mesh axis runs over, the one named last changes fastest.
Arguments:
- inputs: bfloat16 [32768, 768], P(('dp', 'row', 'col')), may hold values from -6 to 6
- segment_ids: int32 [32768], P(('dp', 'row', 'col')), may hold values from 0 to 3, as said below
- query_weight: bfloat16 [768, 768], P('row', 'col'), may hold values from -0.21875 to 0.21875
- key_weight: bfloat16 [768, 768], P('row', 'col'), may hold values from -0.21875 to 0.21875
- value_weight: bfloat16 [768, 768], P('row', 'col'), may hold values from -0.21875 to 0.21875
- output_weight: bfloat16 [768, 768], P('row', 'col'), may hold values from -1.75 to 1.75
- gate_weight: bfloat16 [768, 2048], P('row', 'col'), may hold values from -0.21875 to 0.21875
- up_weight: bfloat16 [768, 2048], P('row', 'col'), may hold values from -0.21875 to 0.21875
- down_weight: bfloat16 [2048, 768], P('row', 'col'), may hold values from -0.125 to 0.125
- first_gain: bfloat16 [768], P(('row', 'col')), may hold values from 0.099609375 to 1.8984375
- second_gain: bfloat16 [768], P(('row', 'col')), may hold values from 0.099609375 to 1.8984375
- cotangent: bfloat16 [32768, 768], P(('dp', 'row', 'col')), may hold values from -6 to 6
Outputs:
- layer_out: bfloat16 [32768, 768], P(('dp', 'row', 'col'))
- input_grad: bfloat16 [32768, 768], P(('dp', 'row', 'col'))
- query_grad: float32 [768, 768], P('row', 'col')
- key_grad: float32 [768, 768], P('row', 'col')
- value_grad: float32 [768, 768], P('row', 'col')
- output_grad: float32 [768, 768], P('row', 'col')
- gate_grad: float32 [768, 2048], P('row', 'col')
- up_grad: float32 [768, 2048], P('row', 'col')
- down_grad: float32 [2048, 768], P('row', 'col')
- first_gain_grad: float32 [768], P(('row', 'col'))
- second_gain_grad: float32 [768], P(('row', 'col'))
Inputs may be any that keep to these rules, and one draw needn't show every extreme that they name: `segment_ids`: within each aligned block of 1024 tokens the ids number that block's sequences 0, 1, ... in order; a block holds 1, 2 or 4 sequences of equal length, and each of the three cases occurs in some block.
All inputs are finite; a program needn't handle non-finite values.
Results may differ from a plain program's by a relative error of at most 0.017.
Values may be sent and summed in bfloat16 or wider, within the bound.
No kernel may reach another device: no remote copies, remote signals or barrier semaphores. Data moves between devices by JAX's collectives and lax.ppermute only.
A program may use at most 192 MiB of HBM per device.

v0:
```python
import jax
import jax.numpy as jnp
from jax import lax
from jax.sharding import PartitionSpec as P

HEAD_DIM = 64


EPSILON = 1e-06
ROPE_BASE = 10000.0
NEGATIVE = -1e30


def for_sending(value):

    def short(part):
        return part.astype(jnp.bfloat16) if part.dtype == jnp.float32 else part

    return jax.tree.map(short, value)


def assemble(stack, grid_rows, grid_cols):
    height = stack.shape[1]
    breadth = stack.shape[2]
    return (
        stack.reshape(grid_rows, grid_cols, height, breadth)
        .transpose(0, 2, 1, 3)
        .reshape(grid_rows * height, grid_cols * breadth)
    )


def disassemble(whole, grid_rows, grid_cols):
    height = whole.shape[0] // grid_rows
    breadth = whole.shape[1] // grid_cols
    return (
        whole.reshape(grid_rows, height, grid_cols, breadth)
        .transpose(0, 2, 1, 3)
        .reshape(grid_rows * grid_cols, height, breadth)
    )


def fetch_attention(
    query_weight, key_weight, value_weight, output_weight, first_gain, grid_rows, grid_cols
):
    pieces = (
        lax.all_gather(query_weight[None], ("row", "col"), axis=0, tiled=True),
        lax.all_gather(key_weight[None], ("row", "col"), axis=0, tiled=True),
        lax.all_gather(value_weight[None], ("row", "col"), axis=0, tiled=True),
        lax.all_gather(output_weight[None], ("row", "col"), axis=0, tiled=True),
        lax.all_gather(first_gain[None], ("row", "col"), axis=0, tiled=True),
    )
    wholes = tuple((assemble(piece, grid_rows, grid_cols) for piece in pieces[:4]))
    return wholes + (pieces[4].reshape(-1).astype(jnp.float32),)


def fetch_feedforward(gate_weight, up_weight, down_weight, second_gain, grid_rows, grid_cols):
    pieces = (
        lax.all_gather(gate_weight[None], ("row", "col"), axis=0, tiled=True),
        lax.all_gather(up_weight[None], ("row", "col"), axis=0, tiled=True),
        lax.all_gather(down_weight[None], ("row", "col"), axis=0, tiled=True),
        lax.all_gather(second_gain[None], ("row", "col"), axis=0, tiled=True),
    )
    wholes = tuple((assemble(piece, grid_rows, grid_cols) for piece in pieces[:3]))
    return wholes + (pieces[3].reshape(-1).astype(jnp.float32),)


def rms_scale(values):
    return lax.rsqrt(jnp.mean(values * values, axis=-1, keepdims=True) + EPSILON)


def rotate(values, cosine, sine):
    half = values.shape[-1] // 2
    front = values[..., :half]
    behind = values[..., half:]
    return jnp.concatenate(
        [front * cosine - behind * sine, behind * cosine + front * sine], axis=-1
    )


def split_heads(values, head_count):
    return values.reshape(values.shape[0], head_count, -1).transpose(1, 0, 2)


def join_heads(values):
    return values.transpose(1, 0, 2).reshape(values.shape[1], -1)


def attend_head(operands, allowed, score_scale):
    queries, keys, values = operands
    scores = jnp.einsum("qd,kd->qk", queries, keys, preferred_element_type=jnp.float32)
    logits = jnp.where(allowed, scores * score_scale, NEGATIVE)
    row_top = jnp.max(logits, axis=1, keepdims=True)
    weights = jnp.exp(logits - row_top)
    row_total = jnp.sum(weights, axis=1, keepdims=True)
    probs_low = (weights / row_total).astype(jnp.bfloat16)
    context = jnp.dot(probs_low, values, preferred_element_type=jnp.float32)
    return (context, row_top[:, 0], row_total[:, 0])


def attend_back(operands, allowed, score_scale):
    queries, keys, values, row_top, row_total, grad_context = operands
    scores = jnp.einsum("qd,kd->qk", queries, keys, preferred_element_type=jnp.float32)
    logits = jnp.where(allowed, scores * score_scale, NEGATIVE)
    probs = jnp.exp(logits - row_top[:, None]) / row_total[:, None]
    probs_low = probs.astype(jnp.bfloat16)
    grad_vals = jnp.einsum("qk,qd->kd", probs_low, grad_context, preferred_element_type=jnp.float32)
    grad_probs = jnp.einsum("qd,kd->qk", grad_context, values, preferred_element_type=jnp.float32)
    inner = jnp.sum(probs * grad_probs, axis=1, keepdims=True)
    grad_scores = (jnp.where(allowed, probs * (grad_probs - inner), 0.0) * score_scale).astype(
        jnp.bfloat16
    )
    grad_qrot = jnp.dot(grad_scores, keys, preferred_element_type=jnp.float32)
    grad_krot = jnp.einsum("qk,qd->kd", grad_scores, queries, preferred_element_type=jnp.float32)
    return (grad_qrot, grad_krot, grad_vals)


def weight_term(left, right):
    return jnp.einsum("ta,tb->ab", left, right, preferred_element_type=jnp.float32)


def back_product(grad, weight):
    return jnp.einsum("tb,ab->ta", grad, weight, preferred_element_type=jnp.float32)


def on_device(
    inputs,
    segment_ids,
    query_weight,
    key_weight,
    value_weight,
    output_weight,
    gate_weight,
    up_weight,
    down_weight,
    first_gain,
    second_gain,
    cotangent,
):
    grid_rows = lax.axis_size("row")
    grid_cols = lax.axis_size("col")
    token_count, model_width = inputs.shape
    head_count = model_width // HEAD_DIM
    score_scale = HEAD_DIM ** (-0.5)
    token_index = jnp.arange(token_count, dtype=jnp.int32)
    same_seq = segment_ids[:, None] == segment_ids[None, :]
    allowed = same_seq & (token_index[None, :] <= token_index[:, None])
    starts = jnp.min(jnp.where(same_seq, token_index[None, :], token_count), axis=1)
    positions = (token_index - starts).astype(jnp.float32)
    frequencies = ROPE_BASE ** (-2.0 * jnp.arange(HEAD_DIM // 2, dtype=jnp.float32) / HEAD_DIM)
    phases = positions[:, None] * frequencies[None, :]
    cosine = jnp.cos(phases)[:, None, :]
    sine = jnp.sin(phases)[:, None, :]
    w_query, w_key, w_value, w_output, gain_one = fetch_attention(
        query_weight, key_weight, value_weight, output_weight, first_gain, grid_rows, grid_cols
    )
    query_flat = jnp.dot(inputs, w_query, preferred_element_type=jnp.float32)
    key_flat = jnp.dot(inputs, w_key, preferred_element_type=jnp.float32)
    value_flat = jnp.dot(inputs, w_value, preferred_element_type=jnp.float32)
    queries = rotate(query_flat.reshape(token_count, head_count, HEAD_DIM), cosine, sine).astype(
        jnp.bfloat16
    )
    keys = rotate(key_flat.reshape(token_count, head_count, HEAD_DIM), cosine, sine).astype(
        jnp.bfloat16
    )
    query_heads = queries.transpose(1, 0, 2)
    key_heads = keys.transpose(1, 0, 2)
    value_heads = split_heads(value_flat.astype(jnp.bfloat16), head_count)

    def head_forward(operands):
        return attend_head(operands, allowed, score_scale)

    contexts, row_tops, row_totals = lax.map(head_forward, (query_heads, key_heads, value_heads))
    context = join_heads(contexts).astype(jnp.bfloat16)
    first_sum = inputs.astype(jnp.float32) + jnp.dot(
        context, w_output, preferred_element_type=jnp.float32
    )
    scale_one = rms_scale(first_sum)
    normed_one = first_sum * scale_one
    normed = normed_one * gain_one
    hidden_in = normed.astype(jnp.bfloat16)
    w_gate, w_up, w_down, gain_two = fetch_feedforward(
        gate_weight, up_weight, down_weight, second_gain, grid_rows, grid_cols
    )
    gate_act = jnp.dot(hidden_in, w_gate, preferred_element_type=jnp.float32)
    up_act = jnp.dot(hidden_in, w_up, preferred_element_type=jnp.float32)
    gate_sigmoid = jax.nn.sigmoid(gate_act)
    hidden = (gate_act * gate_sigmoid * up_act).astype(jnp.bfloat16)
    second_sum = normed + jnp.dot(hidden, w_down, preferred_element_type=jnp.float32)
    scale_two = rms_scale(second_sum)
    normed_two = second_sum * scale_two
    layer_out = (normed_two * gain_two).astype(jnp.bfloat16)
    grad_out = cotangent.astype(jnp.float32)
    gain_two_term = jnp.sum(grad_out * normed_two, axis=0)
    grad_norm_two = grad_out * gain_two
    grad_second = scale_two * (
        grad_norm_two - normed_two * jnp.mean(grad_norm_two * normed_two, axis=-1, keepdims=True)
    )
    grad_branch_two = grad_second.astype(jnp.bfloat16)
    w_gate, w_up, w_down, gain_two = fetch_feedforward(
        gate_weight, up_weight, down_weight, second_gain, grid_rows, grid_cols
    )
    down_term = weight_term(hidden, grad_branch_two)
    grad_hidden = back_product(grad_branch_two, w_down)
    grad_gate = (
        grad_hidden * up_act * (gate_sigmoid + gate_act * gate_sigmoid * (1.0 - gate_sigmoid))
    ).astype(jnp.bfloat16)
    grad_up = (grad_hidden * gate_act * gate_sigmoid).astype(jnp.bfloat16)
    gate_term = weight_term(hidden_in, grad_gate)
    up_term = weight_term(hidden_in, grad_up)
    grad_normed = grad_second + back_product(grad_gate, w_gate) + back_product(grad_up, w_up)
    gain_lanes = gain_two_term.reshape(grid_rows * grid_cols, -1)
    feed_shares = (
        lax.psum_scatter(
            disassemble(gate_term, grid_rows, grid_cols),
            ("row", "col"),
            scatter_dimension=0,
            tiled=True,
        ),
        lax.psum_scatter(
            disassemble(up_term, grid_rows, grid_cols),
            ("row", "col"),
            scatter_dimension=0,
            tiled=True,
        ),
        lax.psum_scatter(
            disassemble(down_term, grid_rows, grid_cols),
            ("row", "col"),
            scatter_dimension=0,
            tiled=True,
        ),
        lax.psum_scatter(gain_lanes, ("row", "col"), scatter_dimension=0, tiled=True),
    )
    gain_one_term = jnp.sum(grad_normed * normed_one, axis=0)
    grad_norm_one = grad_normed * gain_one
    grad_first = scale_one * (
        grad_norm_one - normed_one * jnp.mean(grad_norm_one * normed_one, axis=-1, keepdims=True)
    )
    grad_branch_one = grad_first.astype(jnp.bfloat16)
    w_query, w_key, w_value, w_output, gain_one = fetch_attention(
        query_weight, key_weight, value_weight, output_weight, first_gain, grid_rows, grid_cols
    )
    output_term = weight_term(context, grad_branch_one)
    grad_context = back_product(grad_branch_one, w_output).astype(jnp.bfloat16)

    def head_backward(operands):
        return attend_back(operands, allowed, score_scale)

    grad_qrots, grad_krots, grad_valss = lax.map(
        head_backward,
        (
            query_heads,
            key_heads,
            value_heads,
            row_tops,
            row_totals,
            split_heads(grad_context, head_count),
        ),
    )
    grad_query = (
        rotate(grad_qrots.transpose(1, 0, 2), cosine, -sine)
        .reshape(token_count, model_width)
        .astype(jnp.bfloat16)
    )
    grad_key = (
        rotate(grad_krots.transpose(1, 0, 2), cosine, -sine)
        .reshape(token_count, model_width)
        .astype(jnp.bfloat16)
    )
    grad_value = join_heads(grad_valss).astype(jnp.bfloat16)
    query_term = weight_term(inputs, grad_query)
    key_term = weight_term(inputs, grad_key)
    value_term = weight_term(inputs, grad_value)
    input_grad = (
        grad_first
        + back_product(grad_query, w_query)
        + back_product(grad_key, w_key)
        + back_product(grad_value, w_value)
    ).astype(jnp.bfloat16)
    attention_parts = (
        disassemble(query_term, grid_rows, grid_cols),
        disassemble(key_term, grid_rows, grid_cols),
        disassemble(value_term, grid_rows, grid_cols),
        disassemble(output_term, grid_rows, grid_cols),
    )
    first_lanes = gain_one_term.reshape(grid_rows * grid_cols, -1)
    attention_shares = lax.psum_scatter(
        attention_parts + (first_lanes,), ("row", "col"), scatter_dimension=0, tiled=True
    )
    shares = attention_shares[:4] + feed_shares[:3] + (attention_shares[4], feed_shares[3])
    summed = jax.tree.map(
        lambda part: part.astype(jnp.float32),
        lax.psum(for_sending(tuple((share[0] for share in shares))), "dp"),
    )
    return (
        layer_out,
        input_grad,
        summed[0],
        summed[1],
        summed[2],
        summed[3],
        summed[4],
        summed[5],
        summed[6],
        summed[7],
        summed[8],
    )


def solution(mesh):
    placed = (
        P(("dp", "row", "col"), None),
        P(("dp", "row", "col")),
        P("row", "col"),
        P("row", "col"),
        P("row", "col"),
        P("row", "col"),
        P("row", "col"),
        P("row", "col"),
        P("row", "col"),
        P(("row", "col")),
        P(("row", "col")),
        P(("dp", "row", "col"), None),
    )
    return jax.shard_map(
        on_device,
        mesh=mesh,
        in_specs=placed,
        out_specs=(
            P(("dp", "row", "col"), None),
            P(("dp", "row", "col"), None),
            P("row", "col"),
            P("row", "col"),
            P("row", "col"),
            P("row", "col"),
            P("row", "col"),
            P("row", "col"),
            P("row", "col"),
            P(("row", "col")),
            P(("row", "col")),
        ),
        check_vma=False,
    )
```

profile of v0, /device:TPU:0, one launch (start us, length us, event | category | flops | bytes accessed | tf_op | source)
XLA Modules:
  0.0 1591.9 jit_solution(5571109859749134416)
XLA Ops:
  18.3 44.5 %all-reduce.5 = (bf16[768]{0:T(1024)(128)(2,1)S(1)}, bf16[768]{0:T(1024)(128)(2,1)S(1)}) all-reduce(bf16[768]{0:T(1024)(128)(2,1)S(1)} %dynamic-update-slice, bf16[768]{0:T(1024)(128)(2,1)S(1)} %dynamic-update-slice.1), channel_id=6, replica_groups=mesh['dp'=2,'row'=4,'col'=4] {'row','col'}, use_global_device_ids=true, to_apply=%add | all-reduce | flops 1536 | bytes 6144
  65.7 5.9 all-gather.19.cloned.1.call-done
  76.7 4.4 fusion.54
  81.1 50.0 %all-gather.17.cloned.1.call-done = bf16[3072,192]{1,0:T(8,128)(2,1)} async-done(((bf16[192,192]{1,0:T(8,128)(2,1)}), bf16[3072,192]{1,0:T(8,128)(2,1)}) %all-gather.17.cloned.1.call-update) | async-done | bytes 1179664 | tf_op jit(solution)/shard_map/all_gather | solution.py:46
  146.1 44.5 %all-gather.21.cloned.1.call-done = bf16[3072,192]{1,0:T(8,128)(2,1)} async-done(((bf16[192,192]{1,0:T(8,128)(2,1)}), bf16[3072,192]{1,0:T(8,128)(2,1)}) %all-gather.21.cloned.1.call-update) | async-done | bytes 1179664 | tf_op jit(solution)/shard_map/all_gather | solution.py:48
  194.7 4.4 convolution_convert_fusion.1
  199.1 4.3 copy.128
  203.4 56.9 %while.32 = (s32[]{:T(128)}, bf16[12,1024,64]{1,2,0:T(8,128)(2,1)S(1)}, f32[12,1024]{1,0:T(8,128)S(1)}, f32[12,1024]{1,0:T(8,128)S(1)}, bf16[12,1024,64]{2,1,0:T...) while((s32[]{:T(128)}, ...), condition=%wide.region_4.5_spmd.clone.clone, body=%wide.region_1.4_spmd.clone.sunk.clone | while | flops 279967744 | bytes 13678685 | solution.py:172
  265.8 3.8 multiply_reduce_fusion.4
  271.4 48.1 %all-gather.25.cloned.1.call-done = bf16[3072,512]{1,0:T(8,128)(2,1)} async-done(((bf16[192,512]{1,0:T(8,128)(2,1)}), bf16[3072,512]{1,0:T(8,128)(2,1)}) %all-gather.25.cloned.1.call-update) | async-done | bytes 3145744 | tf_op jit(solution)/shard_map/all_gather | solution.py:58
  319.5 4.3 copy.132
  326.6 62.2 %all-gather.27.cloned.1.call-done = bf16[3072,512]{1,0:T(8,128)(2,1)} async-done(((bf16[192,512]{1,0:T(8,128)(2,1)}), bf16[3072,512]{1,0:T(8,128)(2,1)}) %all-gather.27.cloned.1.call-update) | async-done | bytes 3145744 | tf_op jit(solution)/shard_map/all_gather | solution.py:59
  388.8 4.3 copy.133
  395.7 65.5 %all-gather.29.cloned.1.call-done = bf16[8192,192]{0,1:T(8,128)(2,1)} async-done(((bf16[512,192]{0,1:T(8,128)(2,1)}), bf16[8192,192]{0,1:T(8,128)(2,1)}) %all-gather.29.cloned.1.call-update) | async-done | bytes 3145744 | tf_op jit(solution)/shard_map/all_gather | solution.py:60
  461.2 6.6 reshape.314
  473.2 3.6 fusion.73
  476.8 7.8 multiply_convert_fusion.3
  484.6 5.7 multiply_reduce_fusion.3
  493.2 12.6 multiply_convert_fusion.1
  505.8 5.5 fusion.74
  511.3 4.6 multiply_reduce_fusion.1
  520.7 3.5 fusion.77
  528.5 155.0 %while.33 = (s32[]{:T(128)}, f32[12,1024,64]{1,2,0:T(8,128)}, f32[12,1024,64]{1,2,0:T(8,128)}, bf16[12,1024,64]{1,2,0:T(8,128)(2,1)S(1)}, bf16[12,1024,64]{2,1,0...) while((s32[]{:T(128)}, f32[12,1024,64]{1,2,0:T(8,128)}, ...), condition=%wide.region_11.12_spmd.clone.clone, body=%wide.region_9.11_spmd.clone.sunk.clone | while | flops 689961984 | bytes 34129008 | solution.py:248
  582.0 3.3 multiply_reduce_fusion.7
  672.4 3.3 multiply_reduce_fusion.7
  683.6 4.4 multiply_subtract_fusion.1
  692.7 4.9 reshape.317
  697.7 4.8 copy.142
  707.3 4.9 reshape.319
  712.2 4.7 copy.143
  721.2 3.7 reshape.321
  729.2 9.4 fusion.58
  738.5 8.5 reshape.328
  747.0 7.4 copy.148
  755.8 7.4 fusion.79
  763.2 8.4 reshape.326
  771.7 7.3 copy.146
  779.1 7.5 fusion.78
  786.6 8.4 reshape.324
  795.0 7.7 copy.145
  803.4 74.5 %all-reduce.4 = (bf16[16,48]{1,0:T(8,128)(2,1)S(1)}, bf16[16,48]{1,0:T(8,128)(2,1)S(1)}) all-reduce(f32[16,48]{1,0:T(8,128)S(1)} %reshape.330, f32[16,48]{1,0:T(8,128)S(1)} %reshape.331), channel_id=18, replica_groups=mesh['dp'=2,'row'=4,'col'=4] {'row','col'}, use_global_device_ids=true, to_apply=%region_27.28.clone | all-reduce | flops 1536 | bytes 9216
  888.4 77.9 %reduce-scatter.10.cloned.1.call-done = f32[1,192,192]{2,1,0:T(8,128)} async-done(((f32[16,192,192]{2,1,0:T(8,128)}), f32[1,192,192]{2,1,0:T(8,128)}) %reduce-scatter.10.cloned.1.call-update) | async-done | bytes 147472 | tf_op jit(solution)/shard_map/reduce_scatter | solution.py:286
  967.9 133.2 %reduce-scatter.12.cloned.1.call-done = f32[1,192,192]{2,1,0:T(8,128)} async-done(((f32[16,192,192]{2,1,0:T(8,128)}), f32[1,192,192]{2,1,0:T(8,128)}) %reduce-scatter.12.cloned.1.call-update) | async-done | bytes 147472 | tf_op jit(solution)/shard_map/reduce_scatter | solution.py:286
  1102.6 148.1 %reduce-scatter.20.cloned.1.call-done = f32[1,512,192]{1,2,0:T(8,128)} async-done(((f32[16,512,192]{1,2,0:T(8,128)}), f32[1,512,192]{1,2,0:T(8,128)}) %reduce-scatter.20.cloned.1.call-update) | async-done | bytes 393232 | tf_op jit(solution)/shard_map/reduce_scatter | solution.py:225
  1252.5 148.5 %reduce-scatter.18.cloned.1.call-done = f32[1,192,512]{2,1,0:T(8,128)} async-done(((f32[16,192,512]{2,1,0:T(8,128)}), f32[1,192,512]{2,1,0:T(8,128)}) %reduce-scatter.18.cloned.1.call-update) | async-done | bytes 393232 | tf_op jit(solution)/shard_map/reduce_scatter | solution.py:219
  1402.7 148.1 %reduce-scatter.16.cloned.1.call-done = f32[1,192,512]{2,1,0:T(8,128)} async-done(((f32[16,192,512]{2,1,0:T(8,128)}), f32[1,192,512]{2,1,0:T(8,128)}) %reduce-scatter.16.cloned.1.call-update) | async-done | bytes 393232 | tf_op jit(solution)/shard_map/reduce_scatter | solution.py:213
  1556.9 7.9 add_convert_fusion
  1569.0 4.7 all-reduce.10.cloned.1.call-done
  (350 shorter events, 330.5 us)
Async XLA Ops:
  7.2 64.4 %all-gather.19.cloned.1.call-start = ((), (), s32[]{:S(2)}) async-start(), calls=%async_computation.15 | async-start | bytes 1671168 | tf_op jit(solution)/shard_map/all_gather | solution.py:47
  7.9 123.2 %all-gather.17.cloned.1.call-start = ((), (), s32[]{:S(2)}) async-start(), calls=%async_computation.14 | async-start | bytes 1671168 | tf_op jit(solution)/shard_map/all_gather | solution.py:46
  8.7 182.0 %all-gather.21.cloned.1.call-start = ((), (), s32[]{:S(2)}) async-start(), calls=%async_computation.16 | async-start | bytes 1671168 | tf_op jit(solution)/shard_map/all_gather | solution.py:48
  9.4 250.9 %all-gather.23.cloned.1.call-start = ((), (), s32[]{:S(2)}) async-start(), calls=%async_computation.17 | async-start | bytes 1671168 | tf_op jit(solution)/shard_map/all_gather | solution.py:49
  10.0 309.5 %all-gather.25.cloned.1.call-start = ((), (), s32[]{:S(2)}) async-start(), calls=%async_computation.18 | async-start | bytes 3342336 | tf_op jit(solution)/shard_map/all_gather | solution.py:58
  10.6 378.2 %all-gather.27.cloned.1.call-start = ((), (), s32[]{:S(2)}) async-start(), calls=%async_computation.19 | async-start | bytes 3342336 | tf_op jit(solution)/shard_map/all_gather | solution.py:59
  11.1 450.0 %all-gather.29.cloned.1.call-start = ((), (), s32[]{:S(2)}) async-start(), calls=%async_computation.20 | async-start | bytes 3342336 | tf_op jit(solution)/shard_map/all_gather | solution.py:60
  11.9 873.2 %reduce-scatter.14.cloned.1.call-start = ((), (), s32[]{:S(2)}) async-start(), calls=%async_computation.10 | async-start | bytes 3342336 | tf_op jit(solution)/shard_map/reduce_scatter | solution.py:286
  12.1 4.4 copy-start.2
  13.8 2.8 copy-start.45
  13.8 4.1 copy-start.46
  13.8 4.3 copy-start.47
  13.8 49.1 %copy-start.17 = (bf16[1024,768]{1,0:T(8,128)(2,1)S(1)}, bf16[1024,768]{1,0:T(8,128)(2,1)}, u32[]{:S(2)}) copy-start(bf16[1024,768]{1,0:T(8,128)(2,1)} %param.27) | copy-start | bytes 4718596
  62.9 453.1 %copy-start.36 = (f32[768]{0:T(1024)}, f32[768]{0:T(1024)S(1)}, u32[]{:S(2)}) copy-start(f32[768]{0:T(1024)S(1)} %convert_element_type.259) | copy-start | bytes 9220
  64.5 12.2 copy-start.18
  65.7 73.4 %copy-start.29 = (f32[1024,32]{0,1:T(8,128)}, f32[1024,32]{0,1:T(8,128)S(1)}, u32[]{:S(2)}) copy-start(f32[1024,32]{0,1:T(8,128)S(1)} %get-tuple-element.394) | copy-start | bytes 393220
  136.3 2.8 copy-start.16
  194.7 4.4 copy-start.12
  199.1 4.3 copy-start.7
  199.1 4.3 copy-start.34
  260.3 5.5 copy-start.5
  269.6 246.4 %copy-start = (f32[1024,768]{0,1:T(8,128)}, f32[1024,768]{0,1:T(8,128)S(1)}, u32[]{:S(2)}) copy-start(f32[1024,768]{0,1:T(8,128)S(1)} %get-tuple-element.398) | copy-start | bytes 9437188
  269.6 246.4 %copy-start.38 = (f32[1024]{0:T(1024)}, f32[1024]{0:T(1024)S(1)}, u32[]{:S(2)}) copy-start(f32[1024]{0:T(1024)S(1)} %add_rsqrt_fusion.1) | copy-start | bytes 12292
  473.2 3.6 copy-start.15
  476.8 7.8 copy-start.48
  484.6 5.7 copy-start.9
  490.3 21.1 %copy-start.13 = (f32[1024,768]{0,1:T(8,128)}, f32[1024,768]{0,1:T(8,128)S(1)}, u32[]{:S(2)}) copy-start(f32[1024,768]{0,1:T(8,128)S(1)} %get-tuple-element.402) | copy-start | bytes 9437188
  493.2 18.2 %copy-start.43 = (f32[1024]{0:T(1024)}, f32[1024]{0:T(1024)S(1)}, u32[]{:S(2)}) copy-start(f32[1024]{0:T(1024)S(1)} %broadcast_multiply_fusion.1) | copy-start | bytes 12292
  505.8 5.6 copy-start.49
  524.2 4.3 copy-start.3
  524.2 362.6 %reduce-scatter.8.cloned.1.call-start = ((), (), s32[]{:S(2)}) async-start(), calls=%async_computation.7 | async-start | bytes 3342336 | tf_op jit(solution)/shard_map/reduce_scatter | solution.py:286
  528.5 155.0 %copy-start.30 = (f32[1024,32]{0,1:T(8,128)S(1)}, f32[1024,32]{0,1:T(8,128)}, u32[]{:S(2)}) copy-start(f32[1024,32]{0,1:T(8,128)} %copy-done.29) | copy-start | bytes 393220
  528.5 155.0 %copy-start.35 = (f32[1024,32]{0,1:T(8,128)S(1)}, f32[1024,32]{0,1:T(8,128)}, u32[]{:S(2)}) copy-start(f32[1024,32]{0,1:T(8,128)} %get-tuple-element.392) | copy-start | bytes 393220
  683.5 33.9 %copy-start.4 = (bf16[12,1024,64]{1,2,0:T(8,128)(2,1)}, bf16[12,1024,64]{1,2,0:T(8,128)(2,1)S(1)}, u32[]{:S(2)}) copy-start(bf16[12,1024,64]{1,2,0:T(8,128)(2,1)S(1)} %get-tuple-element.119) | copy-start | bytes 4718596
  702.5 263.8 %reduce-scatter.10.cloned.1.call-start = ((), (), s32[]{:S(2)}) async-start(), calls=%async_computation.8 | async-start | bytes 3342336 | tf_op jit(solution)/shard_map/reduce_scatter | solution.py:286
  717.0 384.1 %reduce-scatter.12.cloned.1.call-start = ((), (), s32[]{:S(2)}) async-start(), calls=%async_computation.9 | async-start | bytes 3342336 | tf_op jit(solution)/shard_map/reduce_scatter | solution.py:286
  727.8 523.0 %reduce-scatter.20.cloned.1.call-start = ((), (), s32[]{:S(2)}) async-start(), calls=%async_computation.13 | async-start | bytes 6684672 | tf_op jit(solution)/shard_map/reduce_scatter | solution.py:225
  754.5 646.5 %reduce-scatter.18.cloned.1.call-start = ((), (), s32[]{:S(2)}) async-start(), calls=%async_computation.12 | async-start | bytes 6684672 | tf_op jit(solution)/shard_map/reduce_scatter | solution.py:219
  779.0 771.7 %reduce-scatter.16.cloned.1.call-start = ((), (), s32[]{:S(2)}) async-start(), calls=%async_computation.11 | async-start | bytes 6684672 | tf_op jit(solution)/shard_map/reduce_scatter | solution.py:213
  802.7 75.9 %copy-start.23 = (bf16[1024,12,64]{0,2,1:T(8,128)(2,1)S(1)}, bf16[1024,12,64]{0,2,1:T(8,128)(2,1)}, u32[]{:S(2)}) copy-start(bf16[1024,12,64]{0,2,1:T(8,128)(2,1)} %copy-done.22) | copy-start | bytes 4718596
  802.7 75.9 %copy-start.32 = (bf16[768,768]{0,1:T(8,128)(2,1)S(1)}, bf16[768,768]{0,1:T(8,128)(2,1)}, u32[]{:S(2)}) copy-start(bf16[768,768]{0,1:T(8,128)(2,1)} %reshape.302) | copy-start | bytes 3538948
  802.7 771.0 %all-reduce.10.cloned.1.call-start = ((), (), s32[]{:S(2)}) async-start(), calls=%async_computation.21 | async-start | bytes 1966080 | tf_op jit(solution)/shard_map/psum | solution.py:292
  878.6 3.2 copy-start.25
  878.6 3.2 copy-start.31
  885.1 671.8 %copy-start.1 = (f32[1024,768]{0,1:T(8,128)S(1)}, f32[1024,768]{0,1:T(8,128)}, u32[]{:S(2)}) copy-start(f32[1024,768]{0,1:T(8,128)} %copy-done) | copy-start | bytes 9437188
  885.1 671.8 %copy-start.37 = (f32[768]{0:T(1024)S(1)}, f32[768]{0:T(1024)}, u32[]{:S(2)}) copy-start(f32[768]{0:T(1024)} %copy-done.36) | copy-start | bytes 9220
  885.1 671.8 %copy-start.39 = (f32[1024]{0:T(1024)S(1)}, f32[1024]{0:T(1024)}, u32[]{:S(2)}) copy-start(f32[1024]{0:T(1024)} %copy-done.38) | copy-start | bytes 12292
  885.1 671.8 %copy-start.41 = (f32[1024]{0:T(1024)S(1)}, f32[1024]{0:T(1024)}, u32[]{:S(2)}) copy-start(f32[1024]{0:T(1024)} %copy-done.40) | copy-start | bytes 12292
  (17 other events, 28.9 us)
Sparse Core Ops, SparseCore 0:
  10.9 60.6 all-gather.18
  74.4 56.6 all-gather.16
  133.9 56.6 all-gather.20
  193.3 56.6 all-gather.22
  252.7 66.7 all-gather.24
  322.2 66.5 all-gather.26
  391.5 69.6 all-gather.28
  524.3 128.8 reduce-scatter.13
  702.6 128.9 reduce-scatter.7
  836.4 129.8 reduce-scatter.9
  971.3 129.7 reduce-scatter.11
  1106.2 144.5 reduce-scatter.19
  1256.0 144.9 reduce-scatter.17
  1406.1 144.6 reduce-scatter.15
  1554.6 19.0 all-reduce.9
where the time goes:
time: 1600 us; the launch traced here: 1590 us
  waiting for transfers between devices  941 us (59%)
  matrix products  290 us (18%)
  local copies, waits for them, and re-layouts  157 us (10%)
  blocking collectives  122 us (8%)
  other arithmetic  64.3 us (4%)
    reduce_scatter x4, waiting for transfers between devices, on_device(): lax.psum_scatter(attention_parts + (first_lanes,), ('row', 'col'), scatte...  211 us
    reduce_scatter x1, waiting for transfers between devices, on_device(): lax.psum_scatter(disassemble(up_term, grid_rows, grid_cols), ('row', 'col...  148 us
    reduce_scatter x1, waiting for transfers between devices, on_device(): lax.psum_scatter(disassemble(down_term, grid_rows, grid_cols), ('row', 'c...  148 us
    reduce_scatter x1, waiting for transfers between devices, on_device(): lax.psum_scatter(disassemble(gate_term, grid_rows, grid_cols), ('row', 'c...  148 us
    unnamed x2, blocking collectives  119 us
    all_gather x1, waiting for transfers between devices, fetch_feedforward(): lax.all_gather(down_weight[None], ('row', 'col'), axis=0, tiled=True)  65.5 us
    all_gather x1, waiting for transfers between devices, fetch_feedforward(): lax.all_gather(up_weight[None], ('row', 'col'), axis=0, tiled=True)  62.2 us
    all_gather x1, waiting for transfers between devices, fetch_attention(): lax.all_gather(query_weight[None], ('row', 'col'), axis=0, tiled=True)  50 us
  transfers between devices with their start and end apart: 15, of which 12 were waited for; matrix products, arithmetic and copies ran while one was open for 27% of the time, Pallas kernels for 0%

commit v1 on v0

v1 whole, which is shorter than its diff:
```python
import jax
import jax.numpy as jnp
from jax import lax
from jax.experimental import pallas as pl
from jax.experimental.pallas import tpu as pltpu
from jax.sharding import PartitionSpec as P

HEAD_DIM = 64
EPSILON = 1e-06
ROPE_BASE = 10000.0
NEGATIVE = -1e30
LOG2E = 1.4426950408889634
QUERY_BLOCK = 256
LANES = 128
BF16 = jnp.bfloat16
F32 = jnp.float32
EVERYWHERE = ("dp", "row", "col")


def dot_nn(left, right):
    return lax.dot_general(left, right, (((1,), (0,)), ((), ())), preferred_element_type=F32)


def dot_nt(left, right):
    return lax.dot_general(left, right, (((1,), (1,)), ((), ())), preferred_element_type=F32)


def bit_count(size):
    return size.bit_length() - 1


def bit_order(grid_rows, grid_cols, core):
    col_bits = [("col", b) for b in range(bit_count(grid_cols))]
    row_bits = [("row", b) for b in range(bit_count(grid_rows))]
    return (col_bits[::-1] + row_bits[::-1]) if core else (col_bits + row_bits)


def step_pairs(grid_rows, grid_cols, step):
    pairs = []
    for core in range(2):
        axis, bit = bit_order(grid_rows, grid_cols, core)[step]
        for row in range(grid_rows):
            for col in range(grid_cols):
                to_row = row ^ (1 << bit) if axis == "row" else row
                to_col = col ^ (1 << bit) if axis == "col" else col
                source = (core * grid_rows + row) * grid_cols + col
                target = (core * grid_rows + to_row) * grid_cols + to_col
                pairs.append((source, target))
    return pairs


def other_core(value):
    return lax.ppermute(value, "dp", [(0, 1), (1, 0)])


def gather_blocks(mine, grid_rows, grid_cols):
    steps = bit_count(grid_rows) + bit_count(grid_cols)
    held = mine[None]
    for step in range(steps):
        came = lax.ppermute(held, EVERYWHERE, step_pairs(grid_rows, grid_cols, step))
        if step < steps - 1:
            held = jnp.concatenate([held, came], axis=0)
    return held, came, other_core(held), other_core(came)


def scatter_blocks(own, other, grid_rows, grid_cols):
    steps = bit_count(grid_rows) + bit_count(grid_cols)
    terms = [own, other_core(other)]
    for step in reversed(range(steps)):
        half = terms[0].shape[0] // 2
        away = sum(term[half:].astype(F32) for term in terms).astype(BF16)
        came = lax.ppermute(away, EVERYWHERE, step_pairs(grid_rows, grid_cols, step))
        terms = [term[:half] for term in terms] + [came]
    mine = sum(term[0].astype(F32) for term in terms).astype(BF16)
    theirs = other_core(mine)
    first = lax.axis_index("dp") == 0
    return jnp.stack([jnp.where(first, mine, theirs), jnp.where(first, theirs, mine)]).astype(F32)


def reversed_bits(value, bits):
    out = 0
    for b in range(bits):
        out = out | (((value >> b) & 1) << (bits - 1 - b))
    return out


def place_of(row, col, place, core, grid_rows, grid_cols):
    far_row = row ^ place[0]
    far_col = col ^ place[1]
    row_bits = bit_count(grid_rows)
    col_bits = bit_count(grid_cols)
    plain = far_col + far_row * grid_cols
    turned = reversed_bits(far_col, col_bits) + reversed_bits(far_row, row_bits) * grid_cols
    return jnp.where(core == 0, plain, turned)


def pack_pair(first, second, odd):
    body_a = jnp.where(odd, first[:, 64:], first[:, :128])
    body_b = jnp.where(odd, second[:, 64:], second[:, :128])
    rest_a = jnp.where(odd, first[:, :64], first[:, 128:])
    rest_b = jnp.where(odd, second[:, :64], second[:, 128:])
    low = jnp.where(odd, rest_b, rest_a)
    high = jnp.where(odd, rest_a, rest_b)
    return jnp.concatenate([body_a, body_b, low, high], axis=1)


def unpack_pair(packed, odd):
    body_a, body_b = packed[:, :128], packed[:, 128:256]
    low, high = packed[:, 256:320], packed[:, 320:384]
    rest_a = jnp.where(odd, high, low)
    rest_b = jnp.where(odd, low, high)
    first = jnp.where(odd, jnp.concatenate([rest_a, body_a], axis=1), jnp.concatenate([body_a, rest_a], axis=1))
    second = jnp.where(odd, jnp.concatenate([rest_b, body_b], axis=1), jnp.concatenate([body_b, rest_b], axis=1))
    return first, second


def halves_of(block, core):
    half = block.shape[0] // 2
    return lax.dynamic_slice_in_dim(block, core * half, half, axis=0)


def pack_attention(query_weight, key_weight, value_weight, core, odd):
    query, key, value = (halves_of(w, core) for w in (query_weight, key_weight, value_weight))
    quarter = value.shape[0] // 2
    return jnp.concatenate(
        [pack_pair(query, key, odd), pack_pair(value[:quarter], value[quarter:], odd)], axis=0
    )


def pack_feed(gate, up, down_turned, output, gain_one, gain_two, core, odd):
    gate, up, down_turned, output = (halves_of(w, core) for w in (gate, up, down_turned, output))
    quarter = output.shape[0] // 2
    packed = pack_pair(output[:quarter], output[quarter:], odd)
    gains = jnp.stack([gain_one, gain_two])
    gains = jnp.pad(gains, ((0, quarter - 2), (0, LANES - gains.shape[1])))
    return jnp.concatenate([gate, up, down_turned, jnp.concatenate([packed, gains], axis=1)], axis=0)


def place_scalars():
    return jnp.stack([lax.axis_index("row"), lax.axis_index("col"), lax.axis_index("dp")]).astype(jnp.int32)


def split_rows(top):
    return lax.broadcasted_iota(jnp.int32, top, 1) < 64


def fill_columns(target, rows, low_even, body_even, low_odd, body_odd, pair, swapped):
    base = 384 * pair
    target[rows, base : base + 128] = body_even
    target[rows, base + 256 : base + 384] = body_odd
    first = split_rows(low_even.shape)
    if swapped:
        mixed = jnp.where(first, low_odd, low_even)
        target[rows, base + 128 : base + 256] = pltpu.roll(mixed.astype(F32), 64, 1).astype(BF16)
    else:
        target[rows, base + 128 : base + 256] = jnp.where(first, low_even, low_odd)


def load_stacks(refs, held, sems):
    count = refs[0].shape[0]
    copies = []
    for k, ref in enumerate(refs):
        copies.append(pltpu.make_async_copy(ref, held.at[k // 2, pl.ds((k % 2) * count, count)], sems.at[k]))
    for copy in copies:
        copy.start()
    for copy in copies:
        copy.wait()


def assemble_attention_body(grid, place, m0, m1, o0, o1, w_query, w_key, w_value, held, sems):
    grid_rows, grid_cols = grid
    load_stacks((m0, m1, o0, o1), held, sems)
    where = (place[0], place[1])
    half = w_query.shape[0] // grid_rows // 2
    quarter = half // 2
    for core in range(2):
        side = core ^ place[2]
        for row in range(grid_rows):
            start = row * 2 * half + core * half
            for pair in range(grid_cols // 2):
                at = [place_of(row, 2 * pair + c, where, core, grid_rows, grid_cols) for c in range(2)]
                even, odd = (held.at[side, p] for p in at)
                top = slice(0, half)
                rows = slice(start, start + half)
                rest_even, rest_odd = even[top, 256:384], odd[top, 256:384]
                fill_columns(w_query, rows, rest_even, even[top, 0:128], rest_odd, odd[top, 0:128], pair, False)
                fill_columns(w_key, rows, rest_even, even[top, 128:256], rest_odd, odd[top, 128:256], pair, True)
                low = slice(half, half + quarter)
                rest_even, rest_odd = even[low, 256:384], odd[low, 256:384]
                rows = slice(start, start + quarter)
                fill_columns(w_value, rows, rest_even, even[low, 0:128], rest_odd, odd[low, 0:128], pair, False)
                rows = slice(start + quarter, start + half)
                fill_columns(w_value, rows, rest_even, even[low, 128:256], rest_odd, odd[low, 128:256], pair, True)


def assemble_attention(stacks, place, grid, width):
    count, height, lanes = stacks[0].shape
    whole = jax.ShapeDtypeStruct((width, width), BF16)
    anywhere = pl.BlockSpec(memory_space=pl.ANY)
    vmem = pl.BlockSpec(memory_space=pltpu.VMEM)
    return pl.pallas_call(
        lambda *refs: assemble_attention_body(grid, *refs),
        in_specs=[pl.BlockSpec(memory_space=pltpu.SMEM)] + [anywhere] * 4,
        out_specs=[vmem] * 3,
        out_shape=[whole] * 3,
        scratch_shapes=[pltpu.VMEM((2, 2 * count, height, lanes), BF16), pltpu.SemaphoreType.DMA((4,))],
        name="assemble_attention",
    )(place, *stacks)


def assemble_feed_body(grid, place, m0, m1, o0, o1, w_gate, w_up, w_down, w_output, gains, held, sems):
    grid_rows, grid_cols = grid
    load_stacks((m0, m1, o0, o1), held, sems)
    where = (place[0], place[1])
    half = w_gate.shape[0] // grid_rows // 2
    span = w_gate.shape[1] // grid_cols
    quarter = half // 2
    share = gains.shape[1] // (grid_rows * grid_cols)
    width = gains.shape[1]
    lane = lax.broadcasted_iota(jnp.int32, (LANES, width), 1)
    spread = (lax.rem(lane, share) == lax.broadcasted_iota(jnp.int32, (LANES, width), 0)).astype(BF16)
    block_of = lax.div(lax.broadcasted_iota(jnp.int32, (16, width), 1), share)
    total = jnp.zeros((16, width), F32)
    for core in range(2):
        side = core ^ place[2]
        for row in range(grid_rows):
            start = row * 2 * half + core * half
            for col in range(grid_cols):
                block = held.at[side, place_of(row, col, where, core, grid_rows, grid_cols)]
                for k, target in enumerate((w_gate, w_up)):
                    target[start : start + half, col * span : (col + 1) * span] = block[k * half : (k + 1) * half, :]
                turned = col * 2 * half + core * half
                w_down[turned : turned + half, row * span : (row + 1) * span] = block[2 * half : 3 * half, :]
            for pair in range(grid_cols // 2):
                at = [place_of(row, 2 * pair + c, where, core, grid_rows, grid_cols) for c in range(2)]
                even, odd = (held.at[side, p] for p in at)
                low = slice(3 * half, 3 * half + quarter)
                rest_even, rest_odd = even[low, 256:384], odd[low, 256:384]
                rows = slice(start, start + quarter)
                fill_columns(w_output, rows, rest_even, even[low, 0:128], rest_odd, odd[low, 0:128], pair, False)
                rows = slice(start + quarter, start + half)
                fill_columns(w_output, rows, rest_even, even[low, 128:256], rest_odd, odd[low, 128:256], pair, True)
                if core == 0:
                    for c, block in enumerate((even, odd)):
                        spreaded = dot_nn(block[3 * half : 3 * half + 16, 384:512], spread)
                        total = total + jnp.where(block_of == row * grid_cols + 2 * pair + c, spreaded, 0.0)
    gains[...] = total[:8]


def assemble_feed(stacks, place, grid, width, hidden):
    count, height, lanes = stacks[0].shape
    anywhere = pl.BlockSpec(memory_space=pl.ANY)
    vmem = pl.BlockSpec(memory_space=pltpu.VMEM)
    return pl.pallas_call(
        lambda *refs: assemble_feed_body(grid, *refs),
        in_specs=[pl.BlockSpec(memory_space=pltpu.SMEM)] + [anywhere] * 4,
        out_specs=[vmem] * 5,
        out_shape=[jax.ShapeDtypeStruct((width, hidden), BF16)] * 3
        + [jax.ShapeDtypeStruct((width, width), BF16), jax.ShapeDtypeStruct((8, width), F32)],
        scratch_shapes=[pltpu.VMEM((2, 2 * count, height, lanes), BF16), pltpu.SemaphoreType.DMA((4,))],
        name="assemble_feed",
    )(place, *stacks)


def swap_halves(values):
    lane = lax.broadcasted_iota(jnp.int32, values.shape, 1)
    back = pltpu.roll(values, 32, 1)
    ahead = pltpu.roll(values, LANES - 32, 1)
    return jnp.where(lax.rem(lane, HEAD_DIM) < HEAD_DIM // 2, ahead, back)


def project_body(x, w_query, w_key, w_value, cosine, sine, query, key, value):
    width = w_query.shape[1]
    step = 256
    for start in range(0, width, step):
        for weight, out in ((w_query, query), (w_key, key)):
            flat = dot_nn(x[...], weight[:, start : start + step])
            for k in range(step // LANES):
                part = flat[:, k * LANES : (k + 1) * LANES]
                turned = part * cosine[...] + swap_halves(part) * sine[...]
                out[:, start + k * LANES : start + (k + 1) * LANES] = turned.astype(BF16)
        value[:, start : start + step] = dot_nn(x[...], w_value[:, start : start + step]).astype(BF16)


def project(x, w_query, w_key, w_value, cosine, sine):
    tokens, width = x.shape
    rows = 256
    tile = pl.BlockSpec((rows, width), lambda i: (i, 0))
    table = pl.BlockSpec((rows, LANES), lambda i: (i, 0))
    whole = pl.BlockSpec((width, width), lambda i: (0, 0))
    return pl.pallas_call(
        project_body,
        grid=(tokens // rows,),
        in_specs=[tile, whole, whole, whole, table, table],
        out_specs=[tile] * 3,
        out_shape=[jax.ShapeDtypeStruct((tokens, width), BF16)] * 3,
        name="project_heads",
    )(x, w_query, w_key, w_value, cosine, sine)


def attention_forward_body(first, q_ref, k_ref, v_ref, context_ref, lse_ref):
    blocks = q_ref.shape[0] // QUERY_BLOCK
    q_turned = (q_ref[...].astype(F32) * HEAD_DIM**-0.5).T.astype(BF16)
    v_turned = v_ref[...].T
    zero = jnp.zeros((HEAD_DIM, QUERY_BLOCK), BF16)
    square = (QUERY_BLOCK, QUERY_BLOCK)
    causal = lax.broadcasted_iota(jnp.int32, square, 0) <= lax.broadcasted_iota(jnp.int32, square, 1)
    lse_ref[...] = jnp.zeros_like(lse_ref)
    for i in range(blocks):
        now = slice(i * QUERY_BLOCK, (i + 1) * QUERY_BLOCK)
        outs = []
        for h in range(2):
            head = slice(h * HEAD_DIM, (h + 1) * HEAD_DIM)
            mine = q_turned[head, now]
            mine = jnp.concatenate([mine, zero] if h == 0 else [zero, mine], axis=0)
            scores = [dot_nn(k_ref[b * QUERY_BLOCK : (b + 1) * QUERY_BLOCK, :], mine) for b in range(i + 1)]
            scores[i] = jnp.where(causal, scores[i], NEGATIVE)
            top = jnp.max(scores[i], axis=0, keepdims=True)
            for b in range(i):
                block_top = jnp.max(scores[b], axis=0, keepdims=True)
                top = jnp.maximum(top, jnp.where(first[i] <= b, block_top, NEGATIVE))
            top = top * LOG2E
            mixed = None
            total = None
            for b in range(i + 1):
                base = top if b == i else top + jnp.where(first[i] <= b, 0.0, -NEGATIVE)
                weights = jnp.exp2(scores[b] * LOG2E - base)
                part_total = jnp.sum(weights, axis=0, keepdims=True)
                part = dot_nn(v_turned[head, b * QUERY_BLOCK : (b + 1) * QUERY_BLOCK], weights.astype(BF16))
                mixed = part if mixed is None else mixed + part
                total = part_total if total is None else total + part_total
            outs.append(mixed * (1.0 / total))
            lse_ref[0, h : h + 1, now] = top + jnp.log2(total)
        context_ref[now, :] = jnp.concatenate(outs, axis=0).T.astype(BF16)


def attention_forward(first, query, key, value):
    tokens, width = query.shape
    pairs = width // LANES
    spec = pl.BlockSpec((tokens, LANES), lambda j, f: (0, j))
    return pl.pallas_call(
        attention_forward_body,
        grid_spec=pltpu.PrefetchScalarGridSpec(
            num_scalar_prefetch=1,
            grid=(pairs,),
            in_specs=[spec] * 3,
            out_specs=[spec, pl.BlockSpec((1, 8, tokens), lambda j, f: (j, 0, 0))],
        ),
        out_shape=[
            jax.ShapeDtypeStruct((tokens, width), BF16),
            jax.ShapeDtypeStruct((pairs, 8, tokens), F32),
        ],
        name="attention_forward",
    )(first, query, key, value)


def attention_backward_body(first, q_ref, k_ref, v_ref, grad_ref, context_ref, lse_ref, cosine, sine, dq_ref, dk_ref, dv_ref, dk_sum, dv_sum):
    blocks = q_ref.shape[0] // QUERY_BLOCK
    scaled = q_ref[...].astype(F32) * HEAD_DIM**-0.5
    q_turned = scaled.T.astype(BF16)
    q_plain = scaled.astype(BF16)
    k_turned = k_ref[...].T
    grad = grad_ref[...]
    grad_turned = grad.T
    inner = (grad.astype(F32) * context_ref[...].astype(F32)).T
    zero = jnp.zeros((HEAD_DIM, QUERY_BLOCK), BF16)
    square = (QUERY_BLOCK, QUERY_BLOCK)
    causal = lax.broadcasted_iota(jnp.int32, square, 0) <= lax.broadcasted_iota(jnp.int32, square, 1)
    low_lanes = lax.broadcasted_iota(jnp.int32, (QUERY_BLOCK, LANES), 1) < HEAD_DIM
    for i in range(blocks):
        now = slice(i * QUERY_BLOCK, (i + 1) * QUERY_BLOCK)
        grads = []
        for h in range(2):
            head = slice(h * HEAD_DIM, (h + 1) * HEAD_DIM)
            own_lanes = low_lanes if h == 0 else jnp.logical_not(low_lanes)
            q_cols, g_cols = (
                jnp.concatenate([part[head, now], zero] if h == 0 else [zero, part[head, now]], axis=0)
                for part in (q_turned, grad_turned)
            )
            q_rows = jnp.where(own_lanes, q_plain[now, :], 0)
            g_rows = jnp.where(own_lanes, grad[now, :], 0)
            delta = jnp.sum(inner[head, now], axis=0, keepdims=True)
            lse = lse_ref[0, h : h + 1, now]
            dq = None
            for b in range(i + 1):
                there = slice(b * QUERY_BLOCK, (b + 1) * QUERY_BLOCK)
                scores = dot_nn(k_ref[there, :], q_cols)
                base = lse if b == i else lse + jnp.where(first[i] <= b, 0.0, -NEGATIVE)
                if b == i:
                    scores = jnp.where(causal, scores, NEGATIVE)
                probs = jnp.exp2(scores * LOG2E - base)
                grad_probs = dot_nn(v_ref[there, :], g_cols)
                grad_scores = (probs * (grad_probs - delta)).astype(BF16)
                dv = dot_nn(probs.astype(BF16), g_rows)
                dk = dot_nn(grad_scores, q_rows)
                if b == i and h == 0:
                    dv_sum[there, :] = dv
                    dk_sum[there, :] = dk
                else:
                    dv_sum[there, :] += dv
                    dk_sum[there, :] += dk
                part = dot_nn(k_turned[head, there], grad_scores)
                dq = part if dq is None else dq + part
            grads.append(dq * HEAD_DIM**-0.5)
        dq = jnp.concatenate(grads, axis=0).T
        dq_ref[now, :] = (dq * cosine[now, :] - swap_halves(dq) * sine[now, :]).astype(BF16)
    dk = dk_sum[...]
    dk_ref[...] = (dk * cosine[...] - swap_halves(dk) * sine[...]).astype(BF16)
    dv_ref[...] = dv_sum[...].astype(BF16)


def attention_backward(first, query, key, value, grad, context, lse, cosine, sine):
    tokens, width = query.shape
    pairs = width // LANES
    spec = pl.BlockSpec((tokens, LANES), lambda j, f: (0, j))
    table = pl.BlockSpec((tokens, LANES), lambda j, f: (0, 0))
    return pl.pallas_call(
        attention_backward_body,
        grid_spec=pltpu.PrefetchScalarGridSpec(
            num_scalar_prefetch=1,
            grid=(pairs,),
            in_specs=[spec] * 5 + [pl.BlockSpec((1, 8, tokens), lambda j, f: (j, 0, 0)), table, table],
            out_specs=[spec] * 3,
            scratch_shapes=[pltpu.VMEM((tokens, LANES), F32)] * 2,
        ),
        out_shape=[jax.ShapeDtypeStruct((tokens, width), BF16)] * 3,
        name="attention_backward",
    )(first, query, key, value, grad, context, lse, cosine, sine)


def middle_body(
    context, x, cotangent, w_output, w_gate, w_up, w_down, gains,
    layer_out, hidden_in_turned, branch_two_turned, context_turned, hidden, grad_gate, grad_up, grad_first, branch_one, grad_context, gain_grads,
    slope, act,
):
    width = x.shape[1]
    span = w_gate.shape[1]
    chunk = 512
    gain_one = gains[0:1, :]
    gain_two = gains[1:2, :]
    context_now = context[...]
    first_sum = x[...].astype(F32) + dot_nn(context_now, w_output[...])
    scale_one = lax.rsqrt(jnp.mean(first_sum * first_sum, axis=1, keepdims=True) + EPSILON)
    normed_one = first_sum * scale_one
    normed = normed_one * gain_one
    hidden_in = normed.astype(BF16)
    second_sum = normed
    for start in range(0, span, chunk):
        cols = slice(start, start + chunk)
        gate_act = dot_nn(hidden_in, w_gate[:, cols])
        up_act = dot_nn(hidden_in, w_up[:, cols])
        sigmoid = jax.nn.sigmoid(gate_act)
        silu = gate_act * sigmoid
        act[:, cols] = silu
        slope[:, cols] = up_act * (sigmoid + silu * (1.0 - sigmoid))
        hidden_now = (silu * up_act).astype(BF16)
        hidden[:, cols] = hidden_now
        second_sum = second_sum + dot_nt(hidden_now, w_down[:, cols])
    scale_two = lax.rsqrt(jnp.mean(second_sum * second_sum, axis=1, keepdims=True) + EPSILON)
    normed_two = second_sum * scale_two
    layer_out[...] = (normed_two * gain_two).astype(BF16)
    grad_out = cotangent[...].astype(F32)
    two_term = jnp.sum(grad_out * normed_two, axis=0, keepdims=True)
    scaled = grad_out * gain_two
    grad_second = scale_two * (scaled - normed_two * jnp.mean(scaled * normed_two, axis=1, keepdims=True))
    branch_two = grad_second.astype(BF16)
    grad_normed = grad_second
    for start in range(0, span, chunk):
        cols = slice(start, start + chunk)
        grad_hidden = dot_nn(branch_two, w_down[:, cols])
        gate_now = (grad_hidden * slope[:, cols]).astype(BF16)
        up_now = (grad_hidden * act[:, cols]).astype(BF16)
        grad_gate[:, cols] = gate_now
        grad_up[:, cols] = up_now
        grad_normed = grad_normed + dot_nt(gate_now, w_gate[:, cols]) + dot_nt(up_now, w_up[:, cols])
    one_term = jnp.sum(grad_normed * normed_one, axis=0, keepdims=True)
    scaled = grad_normed * gain_one
    first_grad = scale_one * (scaled - normed_one * jnp.mean(scaled * normed_one, axis=1, keepdims=True))
    grad_first[...] = first_grad
    one_now = first_grad.astype(BF16)
    branch_one[...] = one_now
    grad_context[...] = dot_nt(one_now, w_output[...]).astype(BF16)
    hidden_in_turned[...] = hidden_in.T
    branch_two_turned[...] = branch_two.T
    context_turned[...] = context_now.T
    terms = jnp.concatenate([one_term, two_term, jnp.zeros((6, width), F32)], axis=0)

    @pl.when(pl.program_id(0) == 0)
    def _():
        gain_grads[...] = terms

    @pl.when(pl.program_id(0) > 0)
    def _():
        gain_grads[...] += terms


def middle(context, x, cotangent, w_output, w_gate, w_up, w_down, gains):
    tokens, width = x.shape
    span = w_gate.shape[1]
    rows = 256
    tile = pl.BlockSpec((rows, width), lambda i: (i, 0))
    wide = pl.BlockSpec((rows, span), lambda i: (i, 0))
    turned = pl.BlockSpec((width, rows), lambda i: (0, i))
    square = pl.BlockSpec((width, width), lambda i: (0, 0), pipeline_mode=pl.Buffered(1))
    whole = pl.BlockSpec((width, span), lambda i: (0, 0), pipeline_mode=pl.Buffered(1))
    eight = pl.BlockSpec((8, width), lambda i: (0, 0))
    flat = jax.ShapeDtypeStruct((tokens, width), BF16)
    flat_turned = jax.ShapeDtypeStruct((width, tokens), BF16)
    broad = jax.ShapeDtypeStruct((tokens, span), BF16)
    return pl.pallas_call(
        middle_body,
        grid=(tokens // rows,),
        in_specs=[tile, tile, tile, square, whole, whole, whole, eight],
        out_specs=[tile, turned, turned, turned, wide, wide, wide, tile, tile, tile, eight],
        out_shape=[
            flat, flat_turned, flat_turned, flat_turned, broad, broad, broad,
            jax.ShapeDtypeStruct((tokens, width), F32), flat, flat, jax.ShapeDtypeStruct((8, width), F32),
        ],
        scratch_shapes=[pltpu.VMEM((rows, span), F32)] * 2,
        name="feed_forward_and_back",
    )(context, x, cotangent, w_output, w_gate, w_up, w_down, gains)


def store_halves(own, other, where, grid, core_here, row, col, rows, lanes, halves):
    grid_rows, grid_cols = grid
    here = core_here == 0
    at_own = place_of(row, col, where, core_here, grid_rows, grid_cols)
    at_other = place_of(row, col, where, 1 - core_here, grid_rows, grid_cols)
    own[at_own, rows, lanes] = jnp.where(here, halves[0], halves[1])
    other[at_other, rows, lanes] = jnp.where(here, halves[1], halves[0])


def rest_tile(first, second, odd):
    low = split_rows(first.shape)
    rolled = pltpu.roll(second, 64, 1)
    return jnp.where(low, rolled, first) if odd else jnp.where(low, first, rolled)


def feed_grads_body(grid, place, hidden_in_turned, branch_two_turned, context_turned, hidden, grad_gate, grad_up, branch_one, gain_grads, own, other):
    grid_rows, grid_cols = grid
    where = (place[0], place[1])
    width = hidden_in_turned.shape[0]
    half = width // grid_rows // 2
    quarter = half // 2
    span = hidden.shape[1]
    col = pl.program_id(0)
    for k, (left, right) in enumerate(
        ((hidden_in_turned, grad_gate), (hidden_in_turned, grad_up), (branch_two_turned, hidden))
    ):
        product = dot_nn(left[...], right[...]).astype(BF16)
        for row in range(grid_rows):
            halves = [product[row * 2 * half + c * half :][:half] for c in range(2)]
            at = (row, col) if k < 2 else (col, row)
            store_halves(own, other, where, grid, place[2], *at, slice(k * half, (k + 1) * half), slice(0, span), halves)

    @pl.when(col == 0)
    def _():
        product = dot_nn(context_turned[...], branch_one[...])
        share = width // (grid_rows * grid_cols)
        lane = lax.broadcasted_iota(jnp.int32, (width, LANES), 0)
        gather = (lax.rem(lane, share) == lax.broadcasted_iota(jnp.int32, (width, LANES), 1)).astype(BF16)
        block_of = lax.div(lax.broadcasted_iota(jnp.int32, (8, width), 1), share)
        sums = gain_grads[...]
        base = 3 * half
        for row in range(grid_rows):
            for c in range(grid_cols):
                tile = 384 * (c // 2)
                odd = c % 2
                bodies, rests = [], []
                for core in range(2):
                    start = row * 2 * half + core * half
                    lanes = slice(tile + 256 * odd, tile + 256 * odd + 128)
                    mid = slice(tile + 128, tile + 256)
                    top, low = slice(start, start + quarter), slice(start + quarter, start + half)
                    bodies.append((product[top, lanes], product[low, lanes]))
                    rests.append(rest_tile(product[top, mid], product[low, mid], odd))
                rows = slice(base, base + quarter)
                for k in range(2):
                    store_halves(own, other, where, grid, place[2], row, c, rows, slice(128 * k, 128 * (k + 1)), [b[k].astype(BF16) for b in bodies])
                store_halves(own, other, where, grid, place[2], row, c, rows, slice(256, 384), [r.astype(BF16) for r in rests])
                picked = jnp.where(block_of == row * grid_cols + c, sums, 0.0).astype(BF16)
                gain = dot_nn(picked, gather)
                gain = jnp.concatenate([gain, jnp.zeros((quarter - 8, LANES), F32)], axis=0).astype(BF16)
                store_halves(own, other, where, grid, place[2], row, c, rows, slice(384, 512), [gain, gain])


def feed_grads(place, grid, hidden_in_turned, branch_two_turned, context_turned, hidden, grad_gate, grad_up, branch_one, gain_grads):
    width, tokens = hidden_in_turned.shape
    grid_rows, grid_cols = grid
    span = hidden.shape[1] // grid_cols
    half = width // grid_rows // 2
    turned = pl.BlockSpec((width, tokens), lambda i, s: (0, 0), pipeline_mode=pl.Buffered(1))
    piece = pl.BlockSpec((tokens, span), lambda i, s: (0, i))
    flat = pl.BlockSpec((tokens, width), lambda i, s: (0, 0), pipeline_mode=pl.Buffered(1))
    eight = pl.BlockSpec((8, width), lambda i, s: (0, 0))
    shape = (grid_rows * grid_cols, 3 * half + half // 2, span)
    out = pl.BlockSpec(shape, lambda i, s: (0, 0, 0), pipeline_mode=pl.Buffered(1))
    return pl.pallas_call(
        lambda *refs: feed_grads_body(grid, *refs),
        grid_spec=pltpu.PrefetchScalarGridSpec(
            num_scalar_prefetch=1,
            grid=(grid_cols,),
            in_specs=[turned] * 3 + [piece] * 3 + [flat, eight],
            out_specs=[out] * 2,
        ),
        out_shape=[jax.ShapeDtypeStruct(shape, BF16)] * 2,
        name="feed_forward_weight_grads",
    )(place, hidden_in_turned, branch_two_turned, context_turned, hidden, grad_gate, grad_up, branch_one, gain_grads)


def attention_grads_body(grid, place, x_turned, grad_query, grad_key, grad_value, own, other):
    grid_rows, grid_cols = grid
    where = (place[0], place[1])
    width = x_turned.shape[0]
    half = width // grid_rows // 2
    quarter = half // 2
    query, key, value = (dot_nn(x_turned[...], g[...]) for g in (grad_query, grad_key, grad_value))
    for row in range(grid_rows):
        for c in range(grid_cols):
            odd = c % 2
            lanes = slice(256 * odd, 256 * odd + 128)
            tile = 384 * (c // 2)
            body = slice(tile + 256 * odd, tile + 256 * odd + 128)
            mid = slice(tile + 128, tile + 256)
            parts = []
            for core in range(2):
                start = row * 2 * half + core * half
                rows = slice(start, start + half)
                top, low = slice(start, start + quarter), slice(start + quarter, start + half)
                pair = (query[rows, body], key[rows, body], rest_tile(query[rows, mid], key[rows, mid], odd))
                last = (value[top, body], value[low, body], rest_tile(value[top, mid], value[low, mid], odd))
                parts.append([p.astype(BF16) for p in pair + last])
            for k in range(3):
                lanes = slice(128 * k, 128 * (k + 1))
                store_halves(own, other, where, grid, place[2], row, c, slice(0, half), lanes, [p[k] for p in parts])
                store_halves(own, other, where, grid, place[2], row, c, slice(half, half + quarter), lanes, [p[3 + k] for p in parts])


def attention_grads(place, grid, x_turned, grad_query, grad_key, grad_value):
    width, tokens = x_turned.shape
    grid_rows, grid_cols = grid
    half = width // grid_rows // 2
    vmem = pl.BlockSpec(memory_space=pltpu.VMEM)
    shape = (grid_rows * grid_cols, half + half // 2, 384)
    return pl.pallas_call(
        lambda *refs: attention_grads_body(grid, *refs),
        in_specs=[pl.BlockSpec(memory_space=pltpu.SMEM)] + [vmem] * 4,
        out_specs=[vmem] * 2,
        out_shape=[jax.ShapeDtypeStruct(shape, BF16)] * 2,
        name="attention_weight_grads",
    )(place, x_turned, grad_query, grad_key, grad_value)


def input_grad_body(grad_first, grad_query, grad_key, grad_value, w_query, w_key, w_value, out):
    total = grad_first[...]
    for grad, weight in ((grad_query, w_query), (grad_key, w_key), (grad_value, w_value)):
        total = total + dot_nt(grad[...], weight[...])
    out[...] = total.astype(BF16)


def input_gradient(grad_first, grad_query, grad_key, grad_value, w_query, w_key, w_value):
    tokens, width = grad_first.shape
    rows = 256
    tile = pl.BlockSpec((rows, width), lambda i: (i, 0))
    whole = pl.BlockSpec((width, width), lambda i: (0, 0), pipeline_mode=pl.Buffered(1))
    return pl.pallas_call(
        input_grad_body,
        grid=(tokens // rows,),
        in_specs=[tile] * 4 + [whole] * 3,
        out_specs=tile,
        out_shape=jax.ShapeDtypeStruct((tokens, width), BF16),
        name="input_gradient",
    )(grad_first, grad_query, grad_key, grad_value, w_query, w_key, w_value)


def gather_plain(block):
    whole = lax.all_gather(block, "col", axis=1, tiled=True)
    return lax.all_gather(whole, "row", axis=0, tiled=True)


def scatter_plain(whole):
    part = lax.psum_scatter(whole.astype(BF16), "row", scatter_dimension=0, tiled=True)
    part = lax.psum_scatter(part, "col", scatter_dimension=1, tiled=True)
    return lax.psum(part, "dp").astype(F32)


def scatter_gain(whole):
    part = lax.psum_scatter(whole.astype(BF16), ("row", "col"), scatter_dimension=0, tiled=True)
    return lax.psum(part, "dp").astype(F32)


def on_device(
    inputs,
    segment_ids,
    query_weight,
    key_weight,
    value_weight,
    output_weight,
    gate_weight,
    up_weight,
    down_weight,
    first_gain,
    second_gain,
    cotangent,
):
    grid = (lax.axis_size("row"), lax.axis_size("col"))
    tokens, width = inputs.shape
    hidden_width = gate_weight.shape[1] * grid[1]
    core = lax.axis_index("dp")
    odd = (lax.axis_index("col") & 1) == 1
    place = place_scalars()
    packs = grid == (4, 4) and query_weight.shape[1] == 192 and gate_weight.shape[1] == 512

    token_index = jnp.arange(tokens, dtype=jnp.int32)
    same = segment_ids[:, None] == segment_ids[None, :]
    starts = jnp.min(jnp.where(same, token_index[None, :], tokens), axis=1)
    positions = (token_index - starts).astype(F32)
    frequencies = ROPE_BASE ** (-2.0 * jnp.arange(HEAD_DIM // 2, dtype=F32) / HEAD_DIM)
    phases = positions[:, None] * frequencies[None, :]
    cosine = jnp.tile(jnp.cos(phases), (1, 4))
    sine = jnp.sin(phases)
    sine = jnp.tile(jnp.concatenate([-sine, sine], axis=1), (1, 2))
    first = starts[::QUERY_BLOCK] // QUERY_BLOCK
    x_turned = inputs.T

    if packs:
        stacks = gather_blocks(pack_attention(query_weight, key_weight, value_weight, core, odd), *grid)
        w_query, w_key, w_value = assemble_attention(stacks, place, grid, width)
        feed = pack_feed(gate_weight, up_weight, down_weight.T, output_weight, first_gain, second_gain, core, odd)
        feed_stacks = gather_blocks(feed, *grid)
        w_gate, w_up, w_down, w_output, gains = assemble_feed(feed_stacks, place, grid, width, hidden_width)
    else:
        w_query, w_key, w_value, w_output = (
            gather_plain(w) for w in (query_weight, key_weight, value_weight, output_weight)
        )
        w_gate, w_up, w_down = gather_plain(gate_weight), gather_plain(up_weight), gather_plain(down_weight).T
        gains = jnp.stack(
            [lax.all_gather(g, ("row", "col"), axis=0, tiled=True).astype(F32) for g in (first_gain, second_gain)]
        )
        gains = jnp.pad(gains, ((0, 6), (0, 0)))

    query, key, value = project(inputs, w_query, w_key, w_value, cosine, sine)
    context, lse = attention_forward(first, query, key, value)
    (
        layer_out, hidden_in_turned, branch_two_turned, context_turned, hidden, grad_gate, grad_up, grad_first, branch_one, grad_context, gain_grads,
    ) = middle(context, inputs, cotangent, w_output, w_gate, w_up, w_down, gains)

    if packs:
        feed_own, feed_other = feed_grads(
            place, grid, hidden_in_turned, branch_two_turned, context_turned, hidden, grad_gate, grad_up, branch_one, gain_grads
        )
        feed_sum = scatter_blocks(feed_own, feed_other, *grid)
    grad_query, grad_key, grad_value = attention_backward(first, query, key, value, grad_context, context, lse, cosine, sine)
    if packs:
        own, other = attention_grads(place, grid, x_turned, grad_query, grad_key, grad_value)
        heads_sum = scatter_blocks(own, other, *grid)
    input_grad = input_gradient(grad_first, grad_query, grad_key, grad_value, w_query, w_key, w_value)

    if packs:
        half = query_weight.shape[0] // 2
        quarter = half // 2
        gate_out, up_out, down_out = (
            jnp.concatenate([feed_sum[c, k * half : (k + 1) * half] for c in range(2)], axis=0) for k in range(3)
        )
        output_parts = [unpack_pair(feed_sum[c, 3 * half :, :384], odd) for c in range(2)]
        output_out = jnp.concatenate([p for pair in output_parts for p in pair], axis=0)
        share = first_gain.shape[0]
        gain_one_out = feed_sum[0, 3 * half, 384 : 384 + share]
        gain_two_out = feed_sum[0, 3 * half + 1, 384 : 384 + share]
        pairs = [unpack_pair(heads_sum[c, :half], odd) for c in range(2)]
        query_out = jnp.concatenate([p[0] for p in pairs], axis=0)
        key_out = jnp.concatenate([p[1] for p in pairs], axis=0)
        values = [unpack_pair(heads_sum[c, half:], odd) for c in range(2)]
        value_out = jnp.concatenate([p for pair in values for p in pair], axis=0)
        down_out = down_out.T
    else:
        query_out, key_out, value_out = (scatter_plain(dot_nn(x_turned, g)) for g in (grad_query, grad_key, grad_value))
        output_out = scatter_plain(dot_nn(context_turned, branch_one))
        gate_out, up_out = (scatter_plain(dot_nn(hidden_in_turned, g)) for g in (grad_gate, grad_up))
        down_out = scatter_plain(dot_nn(branch_two_turned, hidden).T)
        gain_one_out, gain_two_out = scatter_gain(gain_grads[0]), scatter_gain(gain_grads[1])
    return (
        layer_out,
        input_grad,
        query_out,
        key_out,
        value_out,
        output_out,
        gate_out,
        up_out,
        down_out,
        gain_one_out,
        gain_two_out,
    )


def solution(mesh):
    tokens = P(("dp", "row", "col"), None)
    block = P("row", "col")
    gain = P(("row", "col"))
    return jax.shard_map(
        on_device,
        mesh=mesh,
        in_specs=(tokens, P(("dp", "row", "col"))) + (block,) * 7 + (gain, gain, tokens),
        out_specs=(tokens, tokens) + (block,) * 7 + (gain, gain),
        check_vma=False,
    )
```

time: 1600 us -> 390 us (0.24)
  waiting for transfers between devices: 941 us -> 160 us
  matrix products: 290 us -> 0 us
  Pallas kernels: 0 us -> 158 us
  local copies, waits for them, and re-layouts: 157 us -> 5.95 us
  blocking collectives: 122 us -> 0 us
  other arithmetic: 64.3 us -> 28.4 us
  starting transfers between devices: 1.17 us -> 36.6 us
    reduce_scatter x7 -> x0, waiting for transfers between devices: 656 us -> none  [the longest x4 211 us: on_device(): lax.psum_scatter(attention_parts + (first_lanes,), ('row', 'col'), scatte...]
    dot_general x105 -> x0, matrix products: 290 us -> none  [the longest x7 39.5 us: back_product(): jnp.einsum('tb,ab->ta', grad, weight, preferred_element_type=jnp.float32)]
    all_gather x7 -> x0, waiting for transfers between devices: 276 us -> none  [the longest x1 65.5 us: fetch_feedforward(): lax.all_gather(down_weight[None], ('row', 'col'), axis=0, tiled=True)]
    ppermute x0 -> x24, waiting for transfers between devices: none -> 160 us  [the longest x8 88.8 us: gather_blocks(): lax.ppermute(held, EVERYWHERE, step_pairs(grid_rows, grid_cols, step))]
    pallas_call x0 -> x9, Pallas kernels: none -> 158 us  [the longest x1 39.3 us: middle(): pl.pallas_call(middle_body, grid=(tokens // rows,), in_specs=[tile, tile,...]
    unnamed x2 -> x0, blocking collectives: 119 us -> none
    reshape x20 -> x0, local copies, waits for them, and re-layouts: 78.5 us -> none  [the longest x6 38.8 us: disassemble(): whole.reshape(grid_rows, height, grid_cols, breadth).transpose(0, 2, 1, 3)]
    transpose x8 -> x0, local copies, waits for them, and re-layouts: 40.6 us -> none  [the longest x6 34.9 us: disassemble(): return whole.reshape(grid_rows, height, grid_cols, breadth).transpose(0,...]
  transfers between devices with their start and end apart: 15 -> 24, of which waited for: 12 -> 16; matrix products, arithmetic and copies ran while one was open for 27% -> 5% of each run, Pallas kernels for 0% -> 22%
where the time goes in v1:
time: 390 us
  waiting for transfers between devices  160 us (41%)
  Pallas kernels  158 us (41%)
  starting transfers between devices  36.6 us (9%)
  other arithmetic  28.4 us (7%)
  local copies, waits for them, and re-layouts  5.95 us (2%)
    ppermute x8, waiting for transfers between devices, gather_blocks(): lax.ppermute(held, EVERYWHERE, step_pairs(grid_rows, grid_cols, step))  88.8 us
    ppermute x8, waiting for transfers between devices, scatter_blocks(): lax.ppermute(away, EVERYWHERE, step_pairs(grid_rows, grid_cols, step))  67.4 us
    pallas_call x1, Pallas kernels, middle(): pl.pallas_call(middle_body, grid=(tokens // rows,), in_specs=[tile, tile,...  39.3 us
    pallas_call x1, Pallas kernels, attention_backward(): pl.pallas_call(attention_backward_body, grid_spec=pltpu.PrefetchScalarGri...  33.7 us
    pallas_call x1, Pallas kernels, attention_forward(): pl.pallas_call(attention_forward_body, grid_spec=pltpu.PrefetchScalarGrid...  23 us
    pallas_call x1, Pallas kernels, feed_grads(): pl.pallas_call(lambda *refs: feed_grads_body(grid, *refs), grid_spec=pltp...  21.5 us
    ppermute x8, starting transfers between devices, gather_blocks(): lax.ppermute(held, EVERYWHERE, step_pairs(grid_rows, grid_cols, step))  19.1 us
    ppermute x8, starting transfers between devices, scatter_blocks(): lax.ppermute(away, EVERYWHERE, step_pairs(grid_rows, grid_cols, step))  16.1 us
  transfers between devices with their start and end apart: 24, of which 16 were waited for; matrix products, arithmetic and copies ran while one was open for 5% of the time, Pallas kernels for 22%

profile of v1, /device:TPU:0, one launch (start us, length us, event | category | flops | bytes accessed | tf_op | source)
XLA Modules:
  0.0 389.7 jit_solution(16042089578184690514)
XLA Ops:
  5.0 3.1 collective-permute-start.6
  8.1 8.5 %collective-permute-done.6 = bf16[1,336,512]{2,1,0:T(8,128)(2,1)S(1)} collective-permute-done((bf16[1,336,512]{2,1,0:T(8,128)(2,1)S(1)}, bf16[1,336,512]{2,1,0:T(8,128)(2,1)S(1)}, u32[]{:S(2)}, u32[]{:S(2)}) %collective-permute-start.6) | collective-permute-done | bytes 344096 | tf_op jit(solution)/shard_map/ppermute | solution.py:60
  16.7 2.4 collective-permute-start.7
  19.1 15.2 %collective-permute-done.7 = bf16[2,336,512]{2,1,0:T(8,128)(2,1)S(1)} collective-permute-done((bf16[2,336,512]{2,1,0:T(8,128)(2,1)S(1)}, bf16[2,336,512]{2,1,0:T(8,128)(2,1)S(1)}, u32[]{:S(2)}, u32[]{:S(2)}) %collective-permute-start.7) | collective-permute-done | bytes 688160 | tf_op jit(solution)/shard_map/ppermute | solution.py:60
  34.5 2.4 collective-permute-start.8
  36.9 16.3 %collective-permute-done.8 = bf16[4,336,512]{2,1,0:T(8,128)(2,1)S(1)} collective-permute-done((bf16[4,336,512]{2,1,0:T(8,128)(2,1)S(1)}, bf16[4,336,512]{2,1,0:T(8,128)(2,1)S(1)}, u32[]{:S(2)}, u32[]{:S(2)}) %collective-permute-start.8) | collective-permute-done | bytes 1376288 | tf_op jit(solution)/shard_map/ppermute | solution.py:60
  53.5 2.1 collective-permute-start.9
  56.0 3.2 collective-permute-start
  59.2 27.5 %collective-permute-done.9.refs_2_ = bf16[8,336,512]{2,1,0:T(8,128)(2,1)} collective-permute-done((bf16[8,336,512]{2,1,0:T(8,128)(2,1)S(1)}, bf16[8,336,512]{2,1,0:T(8,128)(2,1)}, u32[]{:S(2)}, u32[]{:S(2)}) %collective-permute-start.9) | collective-permute-done | bytes 2752544 | tf_op jit(solution)/shard_map/ppermute | solution.py:60
  86.8 1.9 collective-permute-start.1
  88.7 5.1 %collective-permute-done.1 = bf16[2,144,384]{2,1,0:T(8,128)(2,1)S(1)} collective-permute-done((bf16[2,144,384]{2,1,0:T(8,128)(2,1)S(1)}, bf16[2,144,384]{2,1,0:T(8,128)(2,1)S(1)}, u32[]{:S(2)}, u32[]{:S(2)}) %collective-permute-start.1) | collective-permute-done | bytes 221216 | tf_op jit(solution)/shard_map/ppermute | solution.py:60
  93.8 2.1 collective-permute-start.2
  95.9 6.3 %collective-permute-done.2 = bf16[4,144,384]{2,1,0:T(8,128)(2,1)S(1)} collective-permute-done((bf16[4,144,384]{2,1,0:T(8,128)(2,1)S(1)}, bf16[4,144,384]{2,1,0:T(8,128)(2,1)S(1)}, u32[]{:S(2)}, u32[]{:S(2)}) %collective-permute-start.2) | collective-permute-done | bytes 442400 | tf_op jit(solution)/shard_map/ppermute | solution.py:60
  102.2 1.0 pad_maximum_fusion.2.refs_1_
  103.2 2.0 collective-permute-start.3
  106.8 9.8 %collective-permute-done.3.refs_2_ = bf16[8,144,384]{2,1,0:T(8,128)(2,1)} collective-permute-done((bf16[8,144,384]{2,1,0:T(8,128)(2,1)}, bf16[8,144,384]{2,1,0:T(8,128)(2,1)}, u32[]{:S(2)}, u32[]{:S(2)}) %collective-permute-start.3) | collective-permute-done | bytes 884768 | tf_op jit(solution)/shard_map/ppermute | solution.py:60
  116.7 1.2 fusion.2
  120.0 1.0 copy.30.sine
  122.2 4.8 %assemble_attention.1 = (bf16[768,768]{1,0:T(8,128)(2,1)}, bf16[768,768]{1,0:T(8,128)(2,1)}, bf16[768,768]{1,0:T(8,128)(2,1)}) custom-call(s32[3]{0:T(128)} %pad_add_fusion.refs_0_, bf16[8,144,384]{2,1,0:T(8,128)(2,1)} %pad_maximum_fusion.2.refs_1_, bf16[8,144,384]{2,1,0:T(8,128)(2,1)} %collective-permute-done.3.refs_2_, ...), custom_call_target="tpu_custom_call" | custom-call | tf_op jit(solution)/shard_map/assemble_attention/pallas_call | solution.py:201
  127.0 8.3 %project_heads.1 = (bf16[1024,768]{1,0:T(8,128)(2,1)}, bf16[1024,768]{1,0:T(8,128)(2,1)}, bf16[1024,768]{1,0:T(8,128)(2,1)}) custom-call(bf16[1024,768]{1,0:T(8,128)(2,1)} %x.5, bf16[768,768]{1,0:T(8,128)(2,1)} %get-tuple-element.42.w_query, bf16[768,768]{1,0:T(8,128)(2,1)} %get-tuple-element.43.w_key, bf16[768,768]{1,0:T(8,128)(2,1)} %get-tuple-element.44.w_value, ...), custom_call_target="tpu_custom_call" | custom-call | tf_op jit(solution)/shard_map/project_heads/pallas_call | solution.py:291
  135.3 23.0 %attention_forward.1 = (bf16[1024,768]{1,0:T(8,128)(2,1)}, f32[6,8,1024]{2,1,0:T(8,128)}) custom-call(s32[4]{0:T(128)} %and_select_fusion.first, bf16[1024,768]{1,0:T(8,128)(2,1)} %get-tuple-element.45.q_ref, bf16[1024,768]{1,0:T(8,128)(2,1)} %get-tuple-element.46.k_ref, bf16[1024,768]{1,0:T(8,128)(2,1)} %get-tuple-element.47.v_ref), custom_call_target="tpu_custom_call" | custom-call | tf_op jit(solution)/shard_map/attention_forward/pallas_call | solution.py:341
  158.2 9.6 %assemble_feed.1 = (bf16[768,2048]{1,0:T(8,128)(2,1)}, bf16[768,2048]{1,0:T(8,128)(2,1)}, bf16[768,2048]{1,0:T(8,128)(2,1)}, bf16[768,768]{1,0:T(8,128)(2,1)}, f32[8,768]{1,0:T(8,128)}) custom-call(s32[3]{0:T(128)} %pad_add_fusion.refs_0_, bf16[8,336,512]{2,1,0:T(8,128)(2,1)} %copy-done.3, bf16[8,336,512]{2,1,0:T(8,128)(2,1)} %collective-permute-done.9.refs_2_, ...), custom_call_target="tpu_custom_call" | custom-call | tf_op jit(solution)/shard_map/assemble_feed/pallas_call | solution.py:254
  167.8 39.3 %feed_forward_and_back.1 = (bf16[1024,768]{1,0:T(8,128)(2,1)}, bf16[768,1024]{1,0:T(8,128)(2,1)}, bf16[768,1024]{1,0:T(8,128)(2,1)}, bf16[768,1024]{1,0:T(8,128)...) custom-call(bf16[1024,768]{1,0:T(8,128)(2,1)} %get-tuple-element.48., ...), custom_call_target="tpu_custom_call" | custom-call | tf_op jit(solution)/shard_map/feed_forward_and_back/pallas_call | solution.py:510
  207.1 21.5 %feed_forward_weight_grads.1 = (bf16[16,336,512]{2,1,0:T(8,128)(2,1)}, bf16[16,336,512]{2,1,0:T(8,128)(2,1)}) custom-call(s32[3]{0:T(128)} %pad_add_fusion.refs_0_, bf16[768,1024]{1,0:T(8,128)(2,1)} %get-tuple-element.63.refs_1_, bf16[768,1024]{1,0:T(8,128)(2,1)} %get-tuple-element.64.refs_2_, bf16[768,1024]{1,0:T(8,128)(2,1)} %get-tuple-element.65.refs_3_, ...), custom_call_target="tpu_custom_call" | custom-call | tf_op jit(solution)/shard_map/feed_forward_weight_grads/pallas_call | solution.py:598
  229.0 1.6 copy.33
  230.6 33.7 %attention_backward.1 = (bf16[1024,768]{1,0:T(8,128)(2,1)}, bf16[1024,768]{1,0:T(8,128)(2,1)}, bf16[1024,768]{1,0:T(8,128)(2,1)}) custom-call(s32[4]{0:T(128)} %and_select_fusion.first, bf16[1024,768]{1,0:T(8,128)(2,1)} %get-tuple-element.45.q_ref, bf16[1024,768]{1,0:T(8,128)(2,1)} %get-tuple-element.46.k_ref, bf16[1024,768]{1,0:T(8,128)(2,1)} %get-tuple-element.47.v_ref, ...), custom_call_target="tpu_custom_call" | custom-call | tf_op jit(solution)/shard_map/attention_backward/pallas_call | solution.py:417
  264.3 8.8 %attention_weight_grads.1 = (bf16[16,144,384]{2,1,0:T(8,128)(2,1)}, bf16[16,144,384]{2,1,0:T(8,128)(2,1)}) custom-call(s32[3]{0:T(128)} %pad_add_fusion.refs_0_, bf16[768,1024]{1,0:T(8,128)(2,1)} %bitcast.56, bf16[1024,768]{1,0:T(8,128)(2,1)} %get-tuple-element.58.grad_query.refs_2_, bf16[1024,768]{1,0:T(8,128)(2,1)} %get-tuple-element.59.grad_key.refs_3_, ...), custom_call_target="tpu_custom_call" | custom-call | tf_op jit(solution)/shard_map/attention_weight_grads/pallas_call | solution.py:645
  273.3 3.8 collective-permute-done.12
  277.1 1.4 add_convert_fusion.2
  278.5 2.1 collective-permute-start.13
  280.6 5.1 %add_convert_fusion = bf16[8,336,512]{2,1,0:T(8,128)(2,1)} fusion(bf16[16,336,512]{2,1,0:T(8,128)(2,1)} %collective-permute-done.18, bf16[16,336,512]{2,1,0:T(8,128)(2,1)} %get-tuple-element.71), kind=kLoop, calls=%fused_computation | loop fusion | flops 5505024 | bytes 8257536 | tf_op jit(solution)/shard_map/convert_element_type | solution.py:71
  285.7 5.9 %collective-permute-done.13 = bf16[8,144,384]{2,1,0:T(8,128)(2,1)S(1)} collective-permute-done((bf16[8,144,384]{2,1,0:T(8,128)(2,1)S(1)}, bf16[8,144,384]{2,1,0:T(8,128)(2,1)S(1)}, u32[]{:S(2)}, u32[]{:S(2)}) %collective-permute-start.13) | collective-permute-done | bytes 884768 | tf_op jit(solution)/shard_map/ppermute | solution.py:72
  291.8 2.1 collective-permute-start.14
  293.8 11.1 %collective-permute-done.14 = bf16[4,144,384]{2,1,0:T(8,128)(2,1)S(1)} collective-permute-done((bf16[4,144,384]{2,1,0:T(8,128)(2,1)S(1)}, bf16[4,144,384]{2,1,0:T(8,128)(2,1)S(1)}, u32[]{:S(2)}, u32[]{:S(2)}) %collective-permute-start.14) | collective-permute-done | bytes 442400 | tf_op jit(solution)/shard_map/ppermute | solution.py:72
  305.1 3.7 collective-permute-start.15
  308.8 5.1 %collective-permute-done.15 = bf16[2,144,384]{2,1,0:T(8,128)(2,1)S(1)} collective-permute-done((bf16[2,144,384]{2,1,0:T(8,128)(2,1)S(1)}, bf16[2,144,384]{2,1,0:T(8,128)(2,1)S(1)}, u32[]{:S(2)}, u32[]{:S(2)}) %collective-permute-start.15) | collective-permute-done | bytes 221216 | tf_op jit(solution)/shard_map/ppermute | solution.py:72
  314.0 5.0 %collective-permute-start.16 = (bf16[1,144,384]{2,1,0:T(8,128)(2,1)S(1)}, bf16[1,144,384]{2,1,0:T(8,128)(2,1)S(1)}, u32[]{:S(2)}, u32[]{:S(2)}) collective-permute-start(bf16[1,144,384]{2,1,0:T(8,128)(2,1)S(1)} %add_convert_fusion.9), channel_id=1, source_target_pairs={{0,1},{1,0},{2,3},{3,2},{4,5},{5,4},{6,7},{7,6},{8,9},{9,8},{10,11... | collective-permute-start | bytes 331784 | tf_op jit(solution)/shard_map/ppermute | solution.py:72
  319.0 2.7 collective-permute-done.16
  321.9 8.6 %input_gradient.1 = bf16[1024,768]{1,0:T(8,128)(2,1)} custom-call(f32[1024,768]{1,0:T(8,128)} %get-tuple-element.55.grad_first, bf16[1024,768]{1,0:T(8,128)(2,1)} %get-tuple-element.58.grad_query.refs_2_, bf16[1024,768]{1,0:T(8,128)(2,1)} %get-tuple-element.59.grad_key.refs_3_, bf16[1024,768]{1,0:T(8,128)(2,1)} %get-tuple-element.60.grad_value.refs_4_, ...), custom_call_target="tpu_custom_call" | custom-call | tf_op jit(solution)/shard_map/input_gradient/pallas_call | solution.py:666
  330.6 2.3 add_convert_fusion.1
  333.0 1.6 collective-permute-start.20
  335.6 15.8 %collective-permute-done.20 = bf16[4,336,512]{2,1,0:T(8,128)(2,1)S(1)} collective-permute-done((bf16[4,336,512]{2,1,0:T(8,128)(2,1)S(1)}, bf16[4,336,512]{2,1,0:T(8,128)(2,1)S(1)}, u32[]{:S(2)}, u32[]{:S(2)}) %collective-permute-start.20) | collective-permute-done | bytes 1376288 | tf_op jit(solution)/shard_map/ppermute | solution.py:72
  351.3 1.7 add_convert_fusion.3
  353.0 1.5 collective-permute-start.21
  354.6 17.7 %collective-permute-done.21 = bf16[2,336,512]{2,1,0:T(8,128)(2,1)S(1)} collective-permute-done((bf16[2,336,512]{2,1,0:T(8,128)(2,1)S(1)}, bf16[2,336,512]{2,1,0:T(8,128)(2,1)S(1)}, u32[]{:S(2)}, u32[]{:S(2)}) %collective-permute-start.21) | collective-permute-done | bytes 688160 | tf_op jit(solution)/shard_map/ppermute | solution.py:72
  372.3 1.3 add_convert_fusion.6
  374.0 9.0 %collective-permute-done.22 = bf16[1,336,512]{2,1,0:T(8,128)(2,1)S(1)} collective-permute-done((bf16[1,336,512]{2,1,0:T(8,128)(2,1)S(1)}, bf16[1,336,512]{2,1,0:T(8,128)(2,1)S(1)}, u32[]{:S(2)}, u32[]{:S(2)}) %collective-permute-start.22) | collective-permute-done | bytes 344096 | tf_op jit(solution)/shard_map/ppermute | solution.py:72
  383.1 1.3 fusion
  (103 shorter events, 18.1 us)
Async XLA Ops:
  0.6 1.7 copy-start
  5.0 11.6 %collective-permute-start.6 = (bf16[1,336,512]{2,1,0:T(8,128)(2,1)S(1)}, bf16[1,336,512]{2,1,0:T(8,128)(2,1)S(1)}, u32[]{:S(2)}, u32[]{:S(2)}) collective-permute-start(bf16[1,336,512]{2,1,0:T(8,128)(2,1)S(1)} %maximum_bitcast_fusion.1), channel_id=1, source_target_pairs={{0,1},{1,0},{2,3},{3,2},{4,5},{5,4},{6,7},{7,6},{8,9},{9,8},{10,11... | collective-permute-start | bytes 1032200 | tf_op jit(solution)/shard_map/ppermute | solution.py:60
  16.7 17.6 %collective-permute-start.7 = (bf16[2,336,512]{2,1,0:T(8,128)(2,1)S(1)}, bf16[2,336,512]{2,1,0:T(8,128)(2,1)S(1)}, u32[]{:S(2)}, u32[]{:S(2)}) collective-permute-start(bf16[2,336,512]{2,1,0:T(8,128)(2,1)S(1)} %pad_maximum_fusion.3), channel_id=1, source_target_pairs={{0,2},{1,3},{2,0},{3,1},{4,6},{5,7},{6,4},{7,5},{8,10},{9,11},{10,... | collective-permute-start | bytes 2064392 | tf_op jit(solution)/shard_map/ppermute | solution.py:60
  34.5 21.1 %copy-start.5 = (bf16[192,192]{1,0:T(8,128)(2,1)S(1)}, bf16[192,192]{1,0:T(8,128)(2,1)}, u32[]{:S(2)}) copy-start(bf16[192,192]{1,0:T(8,128)(2,1)} %param.16) | copy-start | bytes 221188
  34.5 21.2 %copy-start.6 = (bf16[192,192]{1,0:T(8,128)(2,1)S(1)}, bf16[192,192]{1,0:T(8,128)(2,1)}, u32[]{:S(2)}) copy-start(bf16[192,192]{1,0:T(8,128)(2,1)} %param.15) | copy-start | bytes 221188
  34.5 21.3 %copy-start.7 = (bf16[192,192]{1,0:T(8,128)(2,1)S(1)}, bf16[192,192]{1,0:T(8,128)(2,1)}, u32[]{:S(2)}) copy-start(bf16[192,192]{1,0:T(8,128)(2,1)} %param.14) | copy-start | bytes 221188
  34.5 18.7 %collective-permute-start.8 = (bf16[4,336,512]{2,1,0:T(8,128)(2,1)S(1)}, bf16[4,336,512]{2,1,0:T(8,128)(2,1)S(1)}, u32[]{:S(2)}, u32[]{:S(2)}) collective-permute-start(bf16[4,336,512]{2,1,0:T(8,128)(2,1)S(1)} %pad_maximum_fusion.1), channel_id=1, source_target_pairs={{0,4},{1,5},{2,6},{3,7},{4,0},{5,1},{6,2},{7,3},{8,12},{9,13},{10,... | collective-permute-start | bytes 4128776 | tf_op jit(solution)/shard_map/ppermute | solution.py:60
  53.5 49.8 %copy-start.3 = (bf16[8,336,512]{2,1,0:T(8,128)(2,1)}, bf16[8,336,512]{2,1,0:T(8,128)(2,1)S(1)}, u32[]{:S(2)}) copy-start(bf16[8,336,512]{2,1,0:T(8,128)(2,1)S(1)} %pad_maximum_fusion.refs_1_) | copy-start | bytes 8257540
  53.5 33.3 %collective-permute-start.9 = (bf16[8,336,512]{2,1,0:T(8,128)(2,1)S(1)}, bf16[8,336,512]{2,1,0:T(8,128)(2,1)}, u32[]{:S(2)}, u32[]{:S(2)}) collective-permute-start(bf16[8,336,512]{2,1,0:T(8,128)(2,1)S(1)} %pad_maximum_fusion.refs_1_), channel_id=1, source_target_pairs={{0,8},{1,9},{2,10},{3,11},{4,12},{5,13},{6,14},{7,15},{8,0},{9,1},... | collective-permute-start | bytes 8257544 | tf_op jit(solution)/shard_map/ppermute | solution.py:60
  55.9 49.3 %copy-start.8 = (s32[1024]{0:T(1024)S(1)}, s32[1024]{0:T(1024)}, u32[]{:S(2)}) copy-start(s32[1024]{0:T(1024)} %param.13) | copy-start | bytes 12292
  56.0 30.7 %collective-permute-start = (bf16[1,144,384]{2,1,0:T(8,128)(2,1)S(1)}, bf16[1,144,384]{2,1,0:T(8,128)(2,1)S(1)}, u32[]{:S(2)}, u32[]{:S(2)}) collective-permute-start(bf16[1,144,384]{2,1,0:T(8,128)(2,1)S(1)} %maximum_bitcast_fusion.2), channel_id=1, source_target_pairs={{0,1},{1,0},{2,3},{3,2},{4,5},{5,4},{6,7},{7,6},{8,9},{9,8},{10,11... | collective-permute-start | bytes 331784 | tf_op jit(solution)/shard_map/ppermute | solution.py:60
  59.2 99.0 %collective-permute-start.10 = (bf16[8,336,512]{2,1,0:T(8,128)(2,1)S(1)}, bf16[8,336,512]{2,1,0:T(8,128)(2,1)}, u32[]{:S(2)}, u32[]{:S(2)}) collective-permute-start(bf16[8,336,512]{2,1,0:T(8,128)(2,1)S(1)} %pad_maximum_fusion.refs_1_), channel_id=1, source_target_pairs={{0,16},{16,0},{1,17},{17,1},{2,18},{18,2},{3,19},{19,3},{4,20},{20... | collective-permute-start | bytes 8257544 | tf_op jit(solution)/shard_map/ppermute | solution.py:53
  86.7 71.5 %collective-permute-start.11 = (bf16[8,336,512]{2,1,0:T(8,128)(2,1)}, bf16[8,336,512]{2,1,0:T(8,128)(2,1)}, u32[]{:S(2)}, u32[]{:S(2)}) collective-permute-start(bf16[8,336,512]{2,1,0:T(8,128)(2,1)} %collective-permute-done.9.refs_2_), channel_id=1, source_target_pairs={{0,16},{16,0},{1,17},{17,1},{2,18},{18,2},{3,19},{19,3},{4,20},{20... | collective-permute-start | bytes 8257544 | tf_op jit(solution)/shard_map/ppermute | solution.py:53
  86.8 7.0 %collective-permute-start.1 = (bf16[2,144,384]{2,1,0:T(8,128)(2,1)S(1)}, bf16[2,144,384]{2,1,0:T(8,128)(2,1)S(1)}, u32[]{:S(2)}, u32[]{:S(2)}) collective-permute-start(bf16[2,144,384]{2,1,0:T(8,128)(2,1)S(1)} %pad_maximum_fusion.8), channel_id=1, source_target_pairs={{0,2},{1,3},{2,0},{3,1},{4,6},{5,7},{6,4},{7,5},{8,10},{9,11},{10,... | collective-permute-start | bytes 663560 | tf_op jit(solution)/shard_map/ppermute | solution.py:60
  93.8 8.4 %collective-permute-start.2 = (bf16[4,144,384]{2,1,0:T(8,128)(2,1)S(1)}, bf16[4,144,384]{2,1,0:T(8,128)(2,1)S(1)}, u32[]{:S(2)}, u32[]{:S(2)}) collective-permute-start(bf16[4,144,384]{2,1,0:T(8,128)(2,1)S(1)} %pad_maximum_fusion.4), channel_id=1, source_target_pairs={{0,4},{1,5},{2,6},{3,7},{4,0},{5,1},{6,2},{7,3},{8,12},{9,13},{10,... | collective-permute-start | bytes 1327112 | tf_op jit(solution)/shard_map/ppermute | solution.py:60
  103.2 13.4 %collective-permute-start.3 = (bf16[8,144,384]{2,1,0:T(8,128)(2,1)}, bf16[8,144,384]{2,1,0:T(8,128)(2,1)}, u32[]{:S(2)}, u32[]{:S(2)}) collective-permute-start(bf16[8,144,384]{2,1,0:T(8,128)(2,1)} %pad_maximum_fusion.2.refs_1_), channel_id=1, source_target_pairs={{0,8},{1,9},{2,10},{3,11},{4,12},{5,13},{6,14},{7,15},{8,0},{9,1},... | collective-permute-start | bytes 2654216 | tf_op jit(solution)/shard_map/ppermute | solution.py:60
  106.1 16.0 %collective-permute-start.4 = (bf16[8,144,384]{2,1,0:T(8,128)(2,1)}, bf16[8,144,384]{2,1,0:T(8,128)(2,1)}, u32[]{:S(2)}, u32[]{:S(2)}) collective-permute-start(bf16[8,144,384]{2,1,0:T(8,128)(2,1)} %pad_maximum_fusion.2.refs_1_), channel_id=1, source_target_pairs={{0,16},{16,0},{1,17},{17,1},{2,18},{18,2},{3,19},{19,3},{4,20},{20... | collective-permute-start | bytes 2654216 | tf_op jit(solution)/shard_map/ppermute | solution.py:53
  116.6 5.6 %collective-permute-start.5 = (bf16[8,144,384]{2,1,0:T(8,128)(2,1)}, bf16[8,144,384]{2,1,0:T(8,128)(2,1)}, u32[]{:S(2)}, u32[]{:S(2)}) collective-permute-start(bf16[8,144,384]{2,1,0:T(8,128)(2,1)} %collective-permute-done.3.refs_2_), channel_id=1, source_target_pairs={{0,16},{16,0},{1,17},{17,1},{2,18},{18,2},{3,19},{19,3},{4,20},{20... | collective-permute-start | bytes 2654216 | tf_op jit(solution)/shard_map/ppermute | solution.py:53
  207.1 21.9 %copy-start.2 = (bf16[1024,768]{1,0:T(8,128)(2,1)S(1)}, bf16[1024,768]{1,0:T(8,128)(2,1)}, u32[]{:S(2)}) copy-start(bf16[1024,768]{1,0:T(8,128)(2,1)} %x.5) | copy-start | bytes 4718596
  228.6 52.0 %collective-permute-start.18 = (bf16[16,336,512]{2,1,0:T(8,128)(2,1)}, bf16[16,336,512]{2,1,0:T(8,128)(2,1)}, u32[]{:S(2)}, u32[]{:S(2)}) collective-permute-start(bf16[16,336,512]{2,1,0:T(8,128)(2,1)} %get-tuple-element.72), channel_id=1, source_target_pairs={{0,16},{16,0},{1,17},{17,1},{2,18},{18,2},{3,19},{19,3},{4,20},{20... | collective-permute-start | bytes 16515080 | tf_op jit(solution)/shard_map/ppermute | solution.py:53
  273.2 3.9 %collective-permute-start.12 = (bf16[16,144,384]{2,1,0:T(8,128)(2,1)}, bf16[16,144,384]{2,1,0:T(8,128)(2,1)S(1)}, u32[]{:S(2)}, u32[]{:S(2)}) collective-permute-start(bf16[16,144,384]{2,1,0:T(8,128)(2,1)} %get-tuple-element.62), channel_id=1, source_target_pairs={{0,16},{16,0},{1,17},{17,1},{2,18},{18,2},{3,19},{19,3},{4,20},{20... | collective-permute-start | bytes 5308424 | tf_op jit(solution)/shard_map/ppermute | solution.py:53
  278.5 13.1 %collective-permute-start.13 = (bf16[8,144,384]{2,1,0:T(8,128)(2,1)S(1)}, bf16[8,144,384]{2,1,0:T(8,128)(2,1)S(1)}, u32[]{:S(2)}, u32[]{:S(2)}) collective-permute-start(bf16[8,144,384]{2,1,0:T(8,128)(2,1)S(1)} %add_convert_fusion.2), channel_id=1, source_target_pairs={{0,8},{1,9},{2,10},{3,11},{4,12},{5,13},{6,14},{7,15},{8,0},{9,1},... | collective-permute-start | bytes 2654216 | tf_op jit(solution)/shard_map/ppermute | solution.py:72
  280.6 11.0 %copy-start.4 = (bf16[16,144,384]{2,1,0:T(8,128)(2,1)S(1)}, bf16[16,144,384]{2,1,0:T(8,128)(2,1)}, u32[]{:S(2)}) copy-start(bf16[16,144,384]{2,1,0:T(8,128)(2,1)} %get-tuple-element.61) | copy-start | bytes 5308420
  285.7 44.9 %collective-permute-start.19 = (bf16[8,336,512]{2,1,0:T(8,128)(2,1)}, bf16[8,336,512]{2,1,0:T(8,128)(2,1)S(1)}, u32[]{:S(2)}, u32[]{:S(2)}) collective-permute-start(bf16[8,336,512]{2,1,0:T(8,128)(2,1)} %add_convert_fusion), channel_id=1, source_target_pairs={{0,8},{1,9},{2,10},{3,11},{4,12},{5,13},{6,14},{7,15},{8,0},{9,1},... | collective-permute-start | bytes 8257544 | tf_op jit(solution)/shard_map/ppermute | solution.py:72
  291.8 13.2 %collective-permute-start.14 = (bf16[4,144,384]{2,1,0:T(8,128)(2,1)S(1)}, bf16[4,144,384]{2,1,0:T(8,128)(2,1)S(1)}, u32[]{:S(2)}, u32[]{:S(2)}) collective-permute-start(bf16[4,144,384]{2,1,0:T(8,128)(2,1)S(1)} %add_convert_fusion.4), channel_id=1, source_target_pairs={{0,4},{1,5},{2,6},{3,7},{4,0},{5,1},{6,2},{7,3},{8,12},{9,13},{10,... | collective-permute-start | bytes 1327112 | tf_op jit(solution)/shard_map/ppermute | solution.py:72
  305.1 8.9 %collective-permute-start.15 = (bf16[2,144,384]{2,1,0:T(8,128)(2,1)S(1)}, bf16[2,144,384]{2,1,0:T(8,128)(2,1)S(1)}, u32[]{:S(2)}, u32[]{:S(2)}) collective-permute-start(bf16[2,144,384]{2,1,0:T(8,128)(2,1)S(1)} %add_convert_fusion.7), channel_id=1, source_target_pairs={{0,2},{1,3},{2,0},{3,1},{4,6},{5,7},{6,4},{7,5},{8,10},{9,11},{10,... | collective-permute-start | bytes 663560 | tf_op jit(solution)/shard_map/ppermute | solution.py:72
  314.0 7.7 %collective-permute-start.16 = (bf16[1,144,384]{2,1,0:T(8,128)(2,1)S(1)}, bf16[1,144,384]{2,1,0:T(8,128)(2,1)S(1)}, u32[]{:S(2)}, u32[]{:S(2)}) collective-permute-start(bf16[1,144,384]{2,1,0:T(8,128)(2,1)S(1)} %add_convert_fusion.9), channel_id=1, source_target_pairs={{0,1},{1,0},{2,3},{3,2},{4,5},{5,4},{6,7},{7,6},{8,9},{9,8},{10,11... | collective-permute-start | bytes 331784 | tf_op jit(solution)/shard_map/ppermute | solution.py:72
  321.8 8.7 %collective-permute-start.17 = (bf16[144,384]{1,0:T(8,128)(2,1)S(1)}, bf16[144,384]{1,0:T(8,128)(2,1)S(1)}, u32[]{:S(2)}, u32[]{:S(2)}) collective-permute-start(bf16[144,384]{1,0:T(8,128)(2,1)S(1)} %fusion.1), channel_id=1, source_target_pairs={{0,16},{16,0},{1,17},{17,1},{2,18},{18,2},{3,19},{19,3},{4,20},{20... | collective-permute-start | bytes 331784 | tf_op jit(solution)/shard_map/ppermute | solution.py:53
  333.0 18.4 %collective-permute-start.20 = (bf16[4,336,512]{2,1,0:T(8,128)(2,1)S(1)}, bf16[4,336,512]{2,1,0:T(8,128)(2,1)S(1)}, u32[]{:S(2)}, u32[]{:S(2)}) collective-permute-start(bf16[4,336,512]{2,1,0:T(8,128)(2,1)S(1)} %add_convert_fusion.1), channel_id=1, source_target_pairs={{0,4},{1,5},{2,6},{3,7},{4,0},{5,1},{6,2},{7,3},{8,12},{9,13},{10,... | collective-permute-start | bytes 4128776 | tf_op jit(solution)/shard_map/ppermute | solution.py:72
  353.0 19.3 %collective-permute-start.21 = (bf16[2,336,512]{2,1,0:T(8,128)(2,1)S(1)}, bf16[2,336,512]{2,1,0:T(8,128)(2,1)S(1)}, u32[]{:S(2)}, u32[]{:S(2)}) collective-permute-start(bf16[2,336,512]{2,1,0:T(8,128)(2,1)S(1)} %add_convert_fusion.3), channel_id=1, source_target_pairs={{0,2},{1,3},{2,0},{3,1},{4,6},{5,7},{6,4},{7,5},{8,10},{9,11},{10,... | collective-permute-start | bytes 2064392 | tf_op jit(solution)/shard_map/ppermute | solution.py:72
  373.6 9.4 %collective-permute-start.22 = (bf16[1,336,512]{2,1,0:T(8,128)(2,1)S(1)}, bf16[1,336,512]{2,1,0:T(8,128)(2,1)S(1)}, u32[]{:S(2)}, u32[]{:S(2)}) collective-permute-start(bf16[1,336,512]{2,1,0:T(8,128)(2,1)S(1)} %add_convert_fusion.6), channel_id=1, source_target_pairs={{0,1},{1,0},{2,3},{3,2},{4,5},{5,4},{6,7},{7,6},{8,9},{9,8},{10,11... | collective-permute-start | bytes 1032200 | tf_op jit(solution)/shard_map/ppermute | solution.py:72
  384.4 1.7 collective-permute-start.23
  387.0 2.7 copy-start.1
